TPU v7x, 32 devices: a whole 2x2x4 slice. The times are simulated.
32 devices in a mesh: dp: 4 (over z), expert: 8 (over y, x, core).
Axes of the slice: x: 2, y: 2, z: 4, core: 2. Of those that a mesh axis runs over, the one named last changes fastest.
Arguments:
- tokens: bfloat16 [6304, 768], P(('dp', 'expert')), may hold values from -6 to 6
- cotangent: bfloat16 [6304, 768], P(('dp', 'expert')), may hold values from -6 to 6
- routes: int32 [6304, 2], P(('dp', 'expert')), may hold values from 0 to 7, all different within a row; in each aligned block of 197 rows (0 to 196, 197 to 393, ...) at most 50 rows name the same one
- priority: int32 [32, 197], P(('dp', 'expert')), may hold values from 0 to 196, each once within a row
- ln_gains: float32 [2, 768], replicated, may hold values from 0.5 to 1.5
- ln_biases: float32 [2, 768], replicated, may hold values from -2 to 2
- qkv_weight: bfloat16 [768, 2304], P('expert'), may hold values from -0.21875 to 0.21875
- out_weight: bfloat16 [768, 768], P('expert'), may hold values from -1.25 to 1.25
- router: float32 [768, 8], replicated, may hold values from -0.21875 to 0.21875
- w_in: bfloat16 [8, 768, 1536], P('expert'), may hold values from -0.21875 to 0.21875
- w_out: bfloat16 [8, 768, 1536], P('expert'), may hold values from -0.21875 to 0.21875
- norm_momentum: float32 [4, 768], replicated, may hold values from -128 to 128
- router_momentum: float32 [768, 8], replicated, may hold values from -6000 to 6000
- qkv_momentum: float32 [768, 2304], P('expert'), may hold values from -1200 to 1200
- out_momentum: float32 [768, 768], P('expert'), may hold values from -600 to 600
- w_in_momentum: float32 [8, 768, 1536], P('expert', 'dp'), may hold values from -180 to 180
- w_out_momentum: float32 [8, 768, 1536], P('expert', 'dp'), may hold values from -180 to 180
Outputs:
- block_out: float32 [6304, 768], P(('dp', 'expert'))
- grad_tokens: float32 [6304, 768], P(('dp', 'expert'))
- grad_norm: float32 [4, 768], replicated
- grad_router: float32 [768, 8], replicated
- grad_qkv: float32 [768, 2304], P('expert')
- grad_out: float32 [768, 768], P('expert')
- grad_w_in: float32 [8, 768, 1536], P('expert', 'dp')
- grad_w_out: float32 [8, 768, 1536], P('expert', 'dp')
- new_norm: float32 [4, 768], replicated
- new_norm_momentum: float32 [4, 768], replicated
- new_router: float32 [768, 8], replicated
- new_router_momentum: float32 [768, 8], replicated
- new_qkv: float32 [768, 2304], P('expert')
- new_qkv_momentum: float32 [768, 2304], P('expert')
- new_out: float32 [768, 768], P('expert')
- new_out_momentum: float32 [768, 768], P('expert')
- new_w_in: float32 [8, 768, 1536], P('expert', 'dp')
- new_w_in_momentum: float32 [8, 768, 1536], P('expert', 'dp')
- new_w_out: float32 [8, 768, 1536], P('expert', 'dp')
- new_w_out_momentum: float32 [8, 768, 1536], P('expert', 'dp')
Inputs may be any that keep to these rules, and one draw needn't show every extreme that they name: `routes`: each row names two different experts. In the rows of one device no expert is named more than 2 * 25 times. `priority`: each row is an ordering of the 197 tokens of one block.
All inputs are finite; a program needn't handle non-finite values.
Results may differ from a plain program's by a relative error of at most 0.011.
Values may be sent and summed in bfloat16 or wider, within the bound.
A program may use at most 128 MiB of HBM per device.

v0:
```python
import math

import jax
import jax.numpy as jnp
from jax import lax
from jax.sharding import PartitionSpec as P

HEADS = 12
NS_STEPS = 5
SEQ = 197


quintic_one = 3.4445
quintic_two = -4.775
quintic_three = 2.0315
decay_rate = 0.9
matrix_rate = 0.2
norm_rate = 0.004
norm_eps = 1e-06
frob_eps = 1e-07
highest = lax.Precision.HIGHEST
contract_last = (((1,), (1,)), ((), ()))
contract_first = (((0,), (0,)), ((), ()))


def gelu_slope(preact):
    return (
        0.5 * (1.0 + lax.erf(preact * 0.7071067811865476))
        + preact * jnp.exp(-0.5 * preact * preact) * 0.3989422804014327
    )


def layer_stats(token_rows, gain, bias):
    centre = token_rows - jnp.mean(token_rows, axis=-1, keepdims=True)
    inverse = lax.rsqrt(jnp.mean(centre * centre, axis=-1, keepdims=True) + norm_eps)
    scaled = centre * inverse
    return (scaled, inverse, scaled * gain + bias)


def slot_index(choice_ids, order_rows, experts, capacity):
    token_count = choice_ids.shape[0]
    ranked = jnp.take(choice_ids, order_rows, axis=0)
    entries = jnp.concatenate([ranked[:, 0], ranked[:, 1]])
    onehot = (entries[:, None] == jnp.arange(experts, dtype=jnp.int32)[None, :]).astype(jnp.int32)
    before = jnp.cumsum(onehot, axis=0) - onehot
    ranked_slots = jnp.sum(before * onehot, axis=1).reshape(2, token_count).T
    slot_values = jnp.zeros((token_count, 2), jnp.int32).at[order_rows].set(ranked_slots)
    return jnp.where(
        slot_values < capacity, choice_ids * capacity + slot_values, experts * capacity
    )


def gates_of(logits, choice_ids):
    chosen = jnp.take_along_axis(logits, choice_ids, axis=1)
    first_gate = jax.nn.sigmoid(chosen[:, 0] - chosen[:, 1])
    return jnp.stack([first_gate, 1.0 - first_gate], axis=1)


def input_grad(base_grad, normed_grad, scaled, inverse, gain):
    lifted = normed_grad * gain
    centred = (
        lifted
        - jnp.mean(lifted, axis=-1, keepdims=True)
        - scaled * jnp.mean(lifted * scaled, axis=-1, keepdims=True)
    )
    return base_grad + inverse * centred


def ortho_tall(matrix):
    iterate = (matrix / (jnp.sqrt(jnp.sum(matrix * matrix)) + frob_eps)).astype(jnp.bfloat16)
    for iteration in range(NS_STEPS):
        gram_matrix = lax.dot_general(
            iterate, iterate, contract_first, preferred_element_type=jnp.float32
        ).astype(jnp.bfloat16)
        mixer_matrix = (
            quintic_two * gram_matrix.astype(jnp.float32)
            + quintic_three * jnp.dot(gram_matrix, gram_matrix, preferred_element_type=jnp.float32)
        ).astype(jnp.bfloat16)
        iterate = (
            quintic_one * iterate.astype(jnp.float32)
            + jnp.dot(iterate, mixer_matrix, preferred_element_type=jnp.float32)
        ).astype(jnp.bfloat16)
    return iterate


def newton_rows(iter_first, iter_second, gather_pair, gram_pair):
    for iteration in range(NS_STEPS):
        full_first, full_second = gather_pair(iter_first, iter_second)
        gram_first = lax.dot_general(
            iter_first, full_first, contract_last, preferred_element_type=jnp.float32
        ).astype(jnp.bfloat16)
        gram_second = lax.dot_general(
            iter_second, full_second, contract_last, preferred_element_type=jnp.float32
        ).astype(jnp.bfloat16)
        whole_first, whole_second = gram_pair(gram_first, gram_second)
        square_first = jnp.dot(gram_first, whole_first, preferred_element_type=jnp.float32)
        square_second = jnp.dot(gram_second, whole_second, preferred_element_type=jnp.float32)
        mixer_first = (
            quintic_two * gram_first.astype(jnp.float32) + quintic_three * square_first
        ).astype(jnp.bfloat16)
        mixer_second = (
            quintic_two * gram_second.astype(jnp.float32) + quintic_three * square_second
        ).astype(jnp.bfloat16)
        iter_first = (
            quintic_one * iter_first.astype(jnp.float32)
            + jnp.dot(mixer_first, full_first, preferred_element_type=jnp.float32)
        ).astype(jnp.bfloat16)
        iter_second = (
            quintic_one * iter_second.astype(jnp.float32)
            + jnp.dot(mixer_second, full_second, preferred_element_type=jnp.float32)
        ).astype(jnp.bfloat16)
    return (iter_first, iter_second)


def split_heads(qkv_rows, image_count, head_width):
    shaped = qkv_rows.reshape(image_count, SEQ, 3, HEADS, head_width)
    return (shaped[:, :, 0], shaped[:, :, 1], shaped[:, :, 2])


def attention_scores(query_rows, key_rows, score_scale):
    return (
        jnp.einsum("ishd,ithd->ihst", query_rows, key_rows, preferred_element_type=jnp.float32)
        * score_scale
    )


def body(
    tokens,
    cotangent,
    routes,
    priority,
    ln_gains,
    ln_biases,
    qkv_weight,
    out_weight,
    router,
    w_in,
    w_out,
    norm_momentum,
    router_momentum,
    qkv_momentum,
    out_momentum,
    w_in_momentum,
    w_out_momentum,
):
    token_count, model_width = tokens.shape
    experts = router.shape[1]
    hidden_units = w_in.shape[2]
    capacity = (token_count + experts - 1) // experts
    slots_all = experts * capacity
    dp_share = model_width // lax.axis_size("dp")
    image_count = token_count // SEQ
    head_width = model_width // HEADS
    score_scale = 1.0 / math.sqrt(head_width)
    first_weight = w_in[0]
    second_weight = w_out[0]
    cot_float = cotangent.astype(jnp.float32)
    full_qkv, full_out = (
        lax.all_gather(qkv_weight, "expert", axis=0, tiled=True),
        lax.all_gather(out_weight, "expert", axis=0, tiled=True),
    )
    token_float = tokens.astype(jnp.float32)
    scaled_one, inverse_one, normed_one = layer_stats(token_float, ln_gains[0], ln_biases[0])
    attn_in = normed_one.astype(jnp.bfloat16)
    qkv_rows = jnp.dot(attn_in, full_qkv, preferred_element_type=jnp.float32).astype(jnp.bfloat16)
    query_rows, key_rows, value_rows = split_heads(qkv_rows, image_count, head_width)
    scores = attention_scores(query_rows, key_rows, score_scale)
    log_total = jnp.log(jnp.sum(jnp.exp(scores), axis=3, keepdims=True))
    attn_probs = jnp.exp(scores - log_total).astype(jnp.bfloat16)
    mixed_rows = (
        jnp.einsum("ihst,ithd->ishd", attn_probs, value_rows, preferred_element_type=jnp.float32)
        .astype(jnp.bfloat16)
        .reshape(token_count, model_width)
    )
    middle_rows = token_float + jnp.dot(mixed_rows, full_out, preferred_element_type=jnp.float32)
    slot_flat = slot_index(routes, priority[0], experts, capacity)
    scaled, inverse, normed = layer_stats(middle_rows, ln_gains[1], ln_biases[1])
    logits = jnp.dot(normed, router, precision=highest)
    gate_values = gates_of(logits, routes)
    position = jnp.arange(slots_all, dtype=jnp.int32)[:, None]
    pick_first = (slot_flat[:, 0][None, :] == position).astype(jnp.float32)
    pick_second = (slot_flat[:, 1][None, :] == position).astype(jnp.float32)
    placing = (pick_first + pick_second).astype(jnp.bfloat16)
    dispatch = (
        jnp.dot(placing, normed.astype(jnp.bfloat16), preferred_element_type=jnp.float32)
        .astype(jnp.bfloat16)
        .reshape(experts, capacity, model_width)
    )
    arrived = lax.all_to_all(dispatch, "expert", split_axis=0, concat_axis=0, tiled=True)
    arrived_rows = arrived.reshape(slots_all, model_width)
    preact_first = jnp.dot(arrived_rows, first_weight, preferred_element_type=jnp.float32)
    active_first = jax.nn.gelu(preact_first, approximate=False).astype(jnp.bfloat16)
    result = lax.dot_general(
        active_first, second_weight, contract_last, preferred_element_type=jnp.float32
    ).astype(jnp.bfloat16)
    returned = lax.all_to_all(
        result.reshape(experts, capacity, model_width),
        "expert",
        split_axis=0,
        concat_axis=0,
        tiled=True,
    )
    picked = (
        jnp.take(
            returned.reshape(slots_all, model_width),
            slot_flat.reshape(-1),
            axis=0,
            mode="fill",
            fill_value=0,
        )
        .reshape(token_count, 2, model_width)
        .astype(jnp.float32)
    )
    block_out = middle_rows + jnp.sum(gate_values[:, :, None] * picked, axis=1)
    gate_grad = jnp.sum(picked * cot_float[:, None, :], axis=2)
    logit_step = gate_values[:, 0] * gate_values[:, 1] * (gate_grad[:, 0] - gate_grad[:, 1])
    columns = jnp.arange(experts, dtype=jnp.int32)[None, :]
    logit_grad = (
        (routes[:, 0:1] == columns).astype(jnp.float32)
        - (routes[:, 1:2] == columns).astype(jnp.float32)
    ) * logit_step[:, None]
    weighting = pick_first * gate_values[:, 0][None, :] + pick_second * gate_values[:, 1][None, :]
    sent_grad = (
        jnp.dot(weighting, cot_float, precision=highest)
        .astype(jnp.bfloat16)
        .reshape(experts, capacity, model_width)
    )
    again_grads, again_rows = (
        lax.all_to_all(sent_grad, "expert", split_axis=0, concat_axis=0, tiled=True),
        lax.all_to_all(dispatch, "expert", split_axis=0, concat_axis=0, tiled=True),
    )
    grad_rows = again_grads.reshape(slots_all, model_width)
    rows_used = again_rows.reshape(slots_all, model_width)
    preact_again = jnp.dot(rows_used, first_weight, preferred_element_type=jnp.float32)
    active = jax.nn.gelu(preact_again, approximate=False).astype(jnp.bfloat16)
    act_grad = jnp.dot(grad_rows, second_weight, preferred_element_type=jnp.float32)
    expert_pre_grad = (act_grad * gelu_slope(preact_again)).astype(jnp.bfloat16)
    row_grad = lax.dot_general(
        expert_pre_grad, first_weight, contract_last, preferred_element_type=jnp.float32
    ).astype(jnp.bfloat16)
    pre_grad, row_grad = (expert_pre_grad, row_grad)
    returned_grad = lax.all_to_all(
        row_grad.reshape(experts, capacity, model_width),
        "expert",
        split_axis=0,
        concat_axis=0,
        tiled=True,
    )
    first_term = lax.dot_general(
        rows_used, pre_grad, contract_first, preferred_element_type=jnp.float32
    )
    second_term = lax.dot_general(
        grad_rows, active, contract_first, preferred_element_type=jnp.float32
    )
    summed = lax.psum_scatter(
        jnp.concatenate([first_term, second_term], axis=1), "dp", scatter_dimension=0, tiled=True
    )
    grad_first = summed[:, :hidden_units]
    grad_second = summed[:, hidden_units:]
    gathered = (
        jnp.take(
            returned_grad.reshape(slots_all, model_width),
            slot_flat.reshape(-1),
            axis=0,
            mode="fill",
            fill_value=0,
        )
        .reshape(token_count, 2, model_width)
        .astype(jnp.float32)
    )
    normed_grad = jnp.sum(gathered, axis=1) + lax.dot_general(
        logit_grad, router, contract_last, precision=highest
    )
    router_local = lax.dot_general(normed, logit_grad, contract_first, precision=highest)
    middle_grad = input_grad(cot_float, normed_grad, scaled, inverse, ln_gains[1])
    middle_rounded = middle_grad.astype(jnp.bfloat16)
    mixed_grad = lax.dot_general(
        middle_rounded, full_out, contract_last, preferred_element_type=jnp.float32
    ).astype(jnp.bfloat16)
    scores_again = attention_scores(query_rows, key_rows, score_scale)
    probs_again = jnp.exp(scores_again - log_total).astype(jnp.bfloat16)
    grad_heads = mixed_grad.reshape(image_count, SEQ, HEADS, head_width)
    value_grad = jnp.einsum(
        "ihst,ishd->ithd", probs_again, grad_heads, preferred_element_type=jnp.float32
    )
    prob_grad = jnp.einsum(
        "ishd,ithd->ihst", grad_heads, value_rows, preferred_element_type=jnp.float32
    )
    prob_float = probs_again.astype(jnp.float32)
    row_delta = jnp.sum(prob_float * prob_grad, axis=3, keepdims=True)
    score_grad = (prob_float * (prob_grad - row_delta) * score_scale).astype(jnp.bfloat16)
    query_grad = jnp.einsum(
        "ihst,ithd->ishd", score_grad, key_rows, preferred_element_type=jnp.float32
    )
    key_grad = jnp.einsum(
        "ihst,ishd->ithd", score_grad, query_rows, preferred_element_type=jnp.float32
    )
    qkv_grad = (
        jnp.stack([query_grad, key_grad, value_grad], axis=2)
        .astype(jnp.bfloat16)
        .reshape(token_count, 3 * model_width)
    )
    attn_in_grad = lax.dot_general(
        qkv_grad, full_qkv, contract_last, preferred_element_type=jnp.float32
    )
    grad_tokens = input_grad(middle_grad, attn_in_grad, scaled_one, inverse_one, ln_gains[0])
    qkv_term = lax.dot_general(
        attn_in, qkv_grad, contract_first, preferred_element_type=jnp.float32
    )
    out_term = lax.dot_general(
        mixed_rows, middle_rounded, contract_first, preferred_element_type=jnp.float32
    )
    attention_share = lax.psum_scatter(
        jnp.concatenate([qkv_term, out_term], axis=1), "expert", scatter_dimension=0, tiled=True
    )
    norm_local = jnp.stack(
        [
            jnp.sum(attn_in_grad * scaled_one, axis=0),
            jnp.sum(normed_grad * scaled, axis=0),
            jnp.sum(attn_in_grad, axis=0),
            jnp.sum(normed_grad, axis=0),
        ]
    )
    moment_first = decay_rate * w_in_momentum[0] + grad_first
    moment_second = decay_rate * w_out_momentum[0] + grad_second
    expert_squares = jnp.stack(
        [jnp.sum(moment_first * moment_first), jnp.sum(moment_second * moment_second)]
    )
    attention_total, squares_total, router_part, norm_part = lax.psum(
        (attention_share, expert_squares, router_local, norm_local), "dp"
    )
    grad_qkv = attention_total[:, : 3 * model_width]
    grad_out = attention_total[:, 3 * model_width :]
    moment_qkv = decay_rate * qkv_momentum + grad_qkv
    moment_out = decay_rate * out_momentum + grad_out
    attention_squares = jnp.stack(
        [jnp.sum(moment_qkv * moment_qkv), jnp.sum(moment_out * moment_out)]
    )
    grad_router, grad_norm, attention_norms = lax.psum(
        (router_part, norm_part, attention_squares), "expert"
    )
    new_norm_momentum = decay_rate * norm_momentum + grad_norm
    new_norm = jnp.concatenate([ln_gains, ln_biases], axis=0) - norm_rate * new_norm_momentum
    new_router_momentum = decay_rate * router_momentum + grad_router
    new_router = router - matrix_rate * ortho_tall(new_router_momentum).astype(jnp.float32)

    def expert_gather(first_rows, second_rows):
        return (
            lax.all_gather(first_rows, "dp", axis=0, tiled=True),
            lax.all_gather(second_rows, "dp", axis=0, tiled=True),
        )

    def expert_grams(first_gram, second_gram):
        return (
            lax.all_gather(first_gram, "dp", axis=0, tiled=True),
            lax.all_gather(second_gram, "dp", axis=0, tiled=True),
        )

    def attention_gather(first_rows, second_rows):
        return (
            lax.all_gather(first_rows, "expert", axis=0, tiled=True),
            lax.all_gather(second_rows, "expert", axis=0, tiled=True),
        )

    def attention_grams(first_gram, second_gram):
        return (
            lax.all_gather(first_gram, "expert", axis=0, tiled=True),
            lax.all_gather(second_gram, "expert", axis=0, tiled=True),
        )

    iter_first = (moment_first / (jnp.sqrt(squares_total[0]) + frob_eps)).astype(jnp.bfloat16)
    iter_second = (moment_second / (jnp.sqrt(squares_total[1]) + frob_eps)).astype(jnp.bfloat16)
    iter_first, iter_second = newton_rows(iter_first, iter_second, expert_gather, expert_grams)
    iter_qkv = (moment_qkv / (jnp.sqrt(attention_norms[0]) + frob_eps)).astype(jnp.bfloat16)
    iter_out = (moment_out / (jnp.sqrt(attention_norms[1]) + frob_eps)).astype(jnp.bfloat16)
    iter_qkv, iter_out = newton_rows(iter_qkv, iter_out, attention_gather, attention_grams)
    row_base = lax.axis_index("dp") * dp_share
    rows_first = lax.dynamic_slice_in_dim(first_weight, row_base, dp_share, 0).astype(jnp.float32)
    rows_second = lax.dynamic_slice_in_dim(second_weight, row_base, dp_share, 0).astype(jnp.float32)
    widen_factor = math.sqrt(max(1.0, hidden_units / model_width))
    new_first = rows_first - matrix_rate * widen_factor * iter_first.astype(jnp.float32)
    new_second = rows_second - matrix_rate * iter_second.astype(jnp.float32)
    new_qkv = qkv_weight.astype(jnp.float32) - matrix_rate * math.sqrt(3.0) * iter_qkv.astype(
        jnp.float32
    )
    new_out = out_weight.astype(jnp.float32) - matrix_rate * iter_out.astype(jnp.float32)
    return (
        block_out,
        grad_tokens,
        grad_norm,
        grad_router,
        grad_qkv,
        grad_out,
        grad_first[None],
        grad_second[None],
        new_norm,
        new_norm_momentum,
        new_router,
        new_router_momentum,
        new_qkv,
        moment_qkv,
        new_out,
        moment_out,
        new_first[None],
        moment_first[None],
        new_second[None],
        moment_second[None],
    )


def solution(mesh):
    in_specs = (
        P(("dp", "expert"), None),
        P(("dp", "expert"), None),
        P(("dp", "expert"), None),
        P(("dp", "expert"), None),
        P(),
        P(),
        P("expert", None),
        P("expert", None),
        P(),
        P("expert", None, None),
        P("expert", None, None),
        P(),
        P(),
        P("expert", None),
        P("expert", None),
        P("expert", "dp", None),
        P("expert", "dp", None),
    )
    out_specs = (
        P(("dp", "expert"), None),
        P(("dp", "expert"), None),
        P(),
        P(),
        P("expert", None),
        P("expert", None),
        P("expert", "dp", None),
        P("expert", "dp", None),
        P(),
        P(),
        P(),
        P(),
        P("expert", None),
        P("expert", None),
        P("expert", None),
        P("expert", None),
        P("expert", "dp", None),
        P("expert", "dp", None),
        P("expert", "dp", None),
        P("expert", "dp", None),
    )
    return jax.shard_map(body, mesh=mesh, in_specs=in_specs, out_specs=out_specs, check_vma=False)
```

profile of v0, /device:TPU:0, one launch (start us, length us, event | category | flops | bytes accessed | tf_op | source)
XLA Modules:
  0.0 1943.0 jit_solution(9800749417993525664)
XLA Ops:
  19.0 27.5 %all-gather.43.cloned.1.call-done = bf16[768,2304]{1,0:T(8,128)(2,1)} async-done(((bf16[96,2304]{1,0:T(8,128)(2,1)}), bf16[768,2304]{1,0:T(8,128)(2,1)}) %all-gather.43.cloned.1.call-update) | async-done | bytes 3538960 | tf_op jit(solution)/shard_map/all_gather | solution.py:159
  55.5 16.8 all-gather.45.cloned.1.call-done
  87.5 5.7 fusion.61
  101.1 4.6 gather_fusion.1
  117.0 4.2 fusion.32
  133.8 8.1 all-to-all-done.3
  165.7 4.1 fusion.92
  172.8 5.0 fusion.94
  177.7 5.0 fusion.93
  185.1 4.2 fusion.352
  189.4 8.1 pad_maximum_fusion
  197.6 76.0 %reduce-scatter.3.cloned.1.call-done = f32[96,3072]{1,0:T(8,128)} async-done(((f32[768,3072]{1,0:T(8,128)}), f32[96,3072]{1,0:T(8,128)}) %reduce-scatter.3.cloned.1.call-update) | async-done | bytes 1179664 | tf_op jit(solution)/shard_map/reduce_scatter | solution.py:313
  275.8 4.6 pad_maximum_fusion.1
  282.8 4.8 fusion.153
  287.7 44.2 %all-reduce.5.cloned.1.call-done = f32[96,3072]{1,0:T(8,128)} async-done(((f32[96,3072]{1,0:T(8,128)}), f32[96,3072]{1,0:T(8,128)}) %all-reduce.5.cloned.1.call-update) | async-done | bytes 1179664 | tf_op jit(solution)/shard_map/psum | solution.py:329
  339.5 155.2 %reduce-scatter.5.cloned.1.call-done = f32[192,3072]{1,0:T(8,128)} async-done(((f32[768,3072]{1,0:T(8,128)}), f32[192,3072]{1,0:T(8,128)}) %reduce-scatter.5.cloned.1.call-update) | async-done | bytes 2359312 | tf_op jit(solution)/shard_map/reduce_scatter | solution.py:255
  494.7 5.3 multiply_reduce_fusion.3
  501.9 20.2 %all-reduce.2 = (f32[4,768]{1,0:T(4,128)}, f32[768,8]{0,1:T(8,128)}, f32[2]{0:T(128)}) all-reduce(f32[4,768]{1,0:T(4,128)S(1)} %pad_maximum_fusion.4, f32[768,8]{0,1:T(8,128)} %fusion.175, f32[2]{0:T(128)} %pad_maximum_fusion.6), channel_id=1, replica_groups=mesh['dp'=4,'expert'=8] {'dp'}, use_global_device_ids=true, to_apply=%region_21.23 | all-reduce | flops 9218 | bytes 73744 | tf_op jit(solution)/shard_map/psum | solution.py:329
  522.1 23.8 %all-reduce.1 = (f32[4,768]{1,0:T(4,128)S(1)}, f32[768,8]{0,1:T(8,128)}, f32[2]{0:T(128)}) all-reduce(f32[4,768]{1,0:T(4,128)} %get-tuple-element.44, f32[768,8]{0,1:T(8,128)} %get-tuple-element.45, f32[2]{0:T(128)} %pad_maximum_fusion.5), channel_id=1, replica_groups=mesh['dp'=4,'expert'=8] {'expert'}, use_global_device_ids=true, to_apply=%region_22.24 | all-reduce | flops 9218 | bytes 73744 | tf_op jit(solution)/shard_map/psum | solution.py:339
  557.6 13.6 all-gather.67.cloned.1.call-done
  573.7 49.6 %all-gather.87.cloned.1.call-done = bf16[768,1536]{1,0:T(8,128)(2,1)} async-done(((bf16[192,1536]{1,0:T(8,128)(2,1)}), bf16[768,1536]{1,0:T(8,128)(2,1)}) %all-gather.87.cloned.1.call-update) | async-done | bytes 2359312 | tf_op jit(solution)/shard_map/all_gather | solution.py:349
  626.7 47.5 %all-gather.107.cloned.1.call-done = bf16[768,1536]{1,0:T(8,128)(2,1)} async-done(((bf16[192,1536]{1,0:T(8,128)(2,1)}), bf16[768,1536]{1,0:T(8,128)(2,1)}) %all-gather.107.cloned.1.call-update) | async-done | bytes 2359312 | tf_op jit(solution)/shard_map/all_gather | solution.py:350
  677.6 31.1 %all-gather.47.cloned.1.call-done = bf16[768,2304]{1,0:T(8,128)(2,1)} async-done(((bf16[96,2304]{1,0:T(8,128)(2,1)}), bf16[768,2304]{1,0:T(8,128)(2,1)}) %all-gather.47.cloned.1.call-update) | async-done | bytes 3538960 | tf_op jit(solution)/shard_map/all_gather | solution.py:361
  712.7 21.7 %all-gather.69.cloned.1.call-done = bf16[768,768]{1,0:T(8,128)(2,1)} async-done(((bf16[96,768]{1,0:T(8,128)(2,1)}), bf16[768,768]{1,0:T(8,128)(2,1)}) %all-gather.69.cloned.1.call-update) | async-done | bytes 1179664 | tf_op jit(solution)/shard_map/all_gather | solution.py:368
  737.0 29.8 %all-gather.89.cloned.1.call-done = bf16[768,768]{1,0:T(8,128)(2,1)} async-done(((bf16[192,768]{1,0:T(8,128)(2,1)}), bf16[768,768]{1,0:T(8,128)(2,1)}) %all-gather.89.cloned.1.call-update) | async-done | bytes 1179664 | tf_op jit(solution)/shard_map/all_gather | solution.py:355
  770.7 27.1 %all-gather.109.cloned.1.call-done = bf16[768,768]{1,0:T(8,128)(2,1)} async-done(((bf16[192,768]{1,0:T(8,128)(2,1)}), bf16[768,768]{1,0:T(8,128)(2,1)}) %all-gather.109.cloned.1.call-update) | async-done | bytes 1179664 | tf_op jit(solution)/shard_map/all_gather | solution.py:356
  797.8 4.2 fusion.20
  802.1 20.8 %all-gather.49.cloned.1.call-done = bf16[768,768]{1,0:T(8,128)(2,1)} async-done(((bf16[96,768]{1,0:T(8,128)(2,1)}), bf16[768,768]{1,0:T(8,128)(2,1)}) %all-gather.49.cloned.1.call-update) | async-done | bytes 1179664 | tf_op jit(solution)/shard_map/all_gather | solution.py:367
  826.2 22.4 %all-gather.71.cloned.1.call-done = bf16[768,768]{1,0:T(8,128)(2,1)} async-done(((bf16[96,768]{1,0:T(8,128)(2,1)}), bf16[768,768]{1,0:T(8,128)(2,1)}) %all-gather.71.cloned.1.call-update) | async-done | bytes 1179664 | tf_op jit(solution)/shard_map/all_gather | solution.py:362
  851.4 49.2 %all-gather.91.cloned.1.call-done = bf16[768,1536]{1,0:T(8,128)(2,1)} async-done(((bf16[192,1536]{1,0:T(8,128)(2,1)}), bf16[768,1536]{1,0:T(8,128)(2,1)}) %all-gather.91.cloned.1.call-update) | async-done | bytes 2359312 | tf_op jit(solution)/shard_map/all_gather | solution.py:349
  904.0 46.8 %all-gather.111.cloned.1.call-done = bf16[768,1536]{1,0:T(8,128)(2,1)} async-done(((bf16[192,1536]{1,0:T(8,128)(2,1)}), bf16[768,1536]{1,0:T(8,128)(2,1)}) %all-gather.111.cloned.1.call-update) | async-done | bytes 2359312 | tf_op jit(solution)/shard_map/all_gather | solution.py:350
  954.2 31.0 %all-gather.51.cloned.1.call-done = bf16[768,2304]{1,0:T(8,128)(2,1)} async-done(((bf16[96,2304]{1,0:T(8,128)(2,1)}), bf16[768,2304]{1,0:T(8,128)(2,1)}) %all-gather.51.cloned.1.call-update) | async-done | bytes 3538960 | tf_op jit(solution)/shard_map/all_gather | solution.py:361
  989.1 22.3 %all-gather.73.cloned.1.call-done = bf16[768,768]{1,0:T(8,128)(2,1)} async-done(((bf16[96,768]{1,0:T(8,128)(2,1)}), bf16[768,768]{1,0:T(8,128)(2,1)}) %all-gather.73.cloned.1.call-update) | async-done | bytes 1179664 | tf_op jit(solution)/shard_map/all_gather | solution.py:368
  1014.0 29.8 %all-gather.93.cloned.1.call-done = bf16[768,768]{1,0:T(8,128)(2,1)} async-done(((bf16[192,768]{1,0:T(8,128)(2,1)}), bf16[768,768]{1,0:T(8,128)(2,1)}) %all-gather.93.cloned.1.call-update) | async-done | bytes 1179664 | tf_op jit(solution)/shard_map/all_gather | solution.py:355
  1047.6 27.1 %all-gather.113.cloned.1.call-done = bf16[768,768]{1,0:T(8,128)(2,1)} async-done(((bf16[192,768]{1,0:T(8,128)(2,1)}), bf16[768,768]{1,0:T(8,128)(2,1)}) %all-gather.113.cloned.1.call-update) | async-done | bytes 1179664 | tf_op jit(solution)/shard_map/all_gather | solution.py:356
  1074.8 4.2 fusion.21
  1079.0 20.8 %all-gather.53.cloned.1.call-done = bf16[768,768]{1,0:T(8,128)(2,1)} async-done(((bf16[96,768]{1,0:T(8,128)(2,1)}), bf16[768,768]{1,0:T(8,128)(2,1)}) %all-gather.53.cloned.1.call-update) | async-done | bytes 1179664 | tf_op jit(solution)/shard_map/all_gather | solution.py:367
  1103.1 22.5 %all-gather.75.cloned.1.call-done = bf16[768,768]{1,0:T(8,128)(2,1)} async-done(((bf16[96,768]{1,0:T(8,128)(2,1)}), bf16[768,768]{1,0:T(8,128)(2,1)}) %all-gather.75.cloned.1.call-update) | async-done | bytes 1179664 | tf_op jit(solution)/shard_map/all_gather | solution.py:362
  1128.3 49.5 %all-gather.95.cloned.1.call-done = bf16[768,1536]{1,0:T(8,128)(2,1)} async-done(((bf16[192,1536]{1,0:T(8,128)(2,1)}), bf16[768,1536]{1,0:T(8,128)(2,1)}) %all-gather.95.cloned.1.call-update) | async-done | bytes 2359312 | tf_op jit(solution)/shard_map/all_gather | solution.py:349
  1181.2 47.4 %all-gather.115.cloned.1.call-done = bf16[768,1536]{1,0:T(8,128)(2,1)} async-done(((bf16[192,1536]{1,0:T(8,128)(2,1)}), bf16[768,1536]{1,0:T(8,128)(2,1)}) %all-gather.115.cloned.1.call-update) | async-done | bytes 2359312 | tf_op jit(solution)/shard_map/all_gather | solution.py:350
  1232.0 31.1 %all-gather.55.cloned.1.call-done = bf16[768,2304]{1,0:T(8,128)(2,1)} async-done(((bf16[96,2304]{1,0:T(8,128)(2,1)}), bf16[768,2304]{1,0:T(8,128)(2,1)}) %all-gather.55.cloned.1.call-update) | async-done | bytes 3538960 | tf_op jit(solution)/shard_map/all_gather | solution.py:361
  1267.1 21.7 %all-gather.77.cloned.1.call-done = bf16[768,768]{1,0:T(8,128)(2,1)} async-done(((bf16[96,768]{1,0:T(8,128)(2,1)}), bf16[768,768]{1,0:T(8,128)(2,1)}) %all-gather.77.cloned.1.call-update) | async-done | bytes 1179664 | tf_op jit(solution)/shard_map/all_gather | solution.py:368
  1291.4 29.7 %all-gather.97.cloned.1.call-done = bf16[768,768]{1,0:T(8,128)(2,1)} async-done(((bf16[192,768]{1,0:T(8,128)(2,1)}), bf16[768,768]{1,0:T(8,128)(2,1)}) %all-gather.97.cloned.1.call-update) | async-done | bytes 1179664 | tf_op jit(solution)/shard_map/all_gather | solution.py:355
  1324.9 27.3 %all-gather.117.cloned.1.call-done = bf16[768,768]{1,0:T(8,128)(2,1)} async-done(((bf16[192,768]{1,0:T(8,128)(2,1)}), bf16[768,768]{1,0:T(8,128)(2,1)}) %all-gather.117.cloned.1.call-update) | async-done | bytes 1179664 | tf_op jit(solution)/shard_map/all_gather | solution.py:356
  1352.2 4.2 fusion.22
  1356.4 20.8 %all-gather.57.cloned.1.call-done = bf16[768,768]{1,0:T(8,128)(2,1)} async-done(((bf16[96,768]{1,0:T(8,128)(2,1)}), bf16[768,768]{1,0:T(8,128)(2,1)}) %all-gather.57.cloned.1.call-update) | async-done | bytes 1179664 | tf_op jit(solution)/shard_map/all_gather | solution.py:367
  1380.6 22.4 %all-gather.79.cloned.1.call-done = bf16[768,768]{1,0:T(8,128)(2,1)} async-done(((bf16[96,768]{1,0:T(8,128)(2,1)}), bf16[768,768]{1,0:T(8,128)(2,1)}) %all-gather.79.cloned.1.call-update) | async-done | bytes 1179664 | tf_op jit(solution)/shard_map/all_gather | solution.py:362
  1405.6 49.6 %all-gather.99.cloned.1.call-done = bf16[768,1536]{1,0:T(8,128)(2,1)} async-done(((bf16[192,1536]{1,0:T(8,128)(2,1)}), bf16[768,1536]{1,0:T(8,128)(2,1)}) %all-gather.99.cloned.1.call-update) | async-done | bytes 2359312 | tf_op jit(solution)/shard_map/all_gather | solution.py:349
  1458.5 47.5 %all-gather.119.cloned.1.call-done = bf16[768,1536]{1,0:T(8,128)(2,1)} async-done(((bf16[192,1536]{1,0:T(8,128)(2,1)}), bf16[768,1536]{1,0:T(8,128)(2,1)}) %all-gather.119.cloned.1.call-update) | async-done | bytes 2359312 | tf_op jit(solution)/shard_map/all_gather | solution.py:350
  1509.4 31.0 %all-gather.59.cloned.1.call-done = bf16[768,2304]{1,0:T(8,128)(2,1)} async-done(((bf16[96,2304]{1,0:T(8,128)(2,1)}), bf16[768,2304]{1,0:T(8,128)(2,1)}) %all-gather.59.cloned.1.call-update) | async-done | bytes 3538960 | tf_op jit(solution)/shard_map/all_gather | solution.py:361
  1544.4 21.9 %all-gather.81.cloned.1.call-done = bf16[768,768]{1,0:T(8,128)(2,1)} async-done(((bf16[96,768]{1,0:T(8,128)(2,1)}), bf16[768,768]{1,0:T(8,128)(2,1)}) %all-gather.81.cloned.1.call-update) | async-done | bytes 1179664 | tf_op jit(solution)/shard_map/all_gather | solution.py:368
  1569.1 29.6 %all-gather.101.cloned.1.call-done = bf16[768,768]{1,0:T(8,128)(2,1)} async-done(((bf16[192,768]{1,0:T(8,128)(2,1)}), bf16[768,768]{1,0:T(8,128)(2,1)}) %all-gather.101.cloned.1.call-update) | async-done | bytes 1179664 | tf_op jit(solution)/shard_map/all_gather | solution.py:355
  1602.5 27.1 %all-gather.121.cloned.1.call-done = bf16[768,768]{1,0:T(8,128)(2,1)} async-done(((bf16[192,768]{1,0:T(8,128)(2,1)}), bf16[768,768]{1,0:T(8,128)(2,1)}) %all-gather.121.cloned.1.call-update) | async-done | bytes 1179664 | tf_op jit(solution)/shard_map/all_gather | solution.py:356
  1629.6 4.2 fusion.23
  1633.9 20.7 %all-gather.61.cloned.1.call-done = bf16[768,768]{1,0:T(8,128)(2,1)} async-done(((bf16[96,768]{1,0:T(8,128)(2,1)}), bf16[768,768]{1,0:T(8,128)(2,1)}) %all-gather.61.cloned.1.call-update) | async-done | bytes 1179664 | tf_op jit(solution)/shard_map/all_gather | solution.py:367
  1657.8 22.5 %all-gather.83.cloned.1.call-done = bf16[768,768]{1,0:T(8,128)(2,1)} async-done(((bf16[96,768]{1,0:T(8,128)(2,1)}), bf16[768,768]{1,0:T(8,128)(2,1)}) %all-gather.83.cloned.1.call-update) | async-done | bytes 1179664 | tf_op jit(solution)/shard_map/all_gather | solution.py:362
  1683.1 49.3 %all-gather.103.cloned.1.call-done = bf16[768,1536]{1,0:T(8,128)(2,1)} async-done(((bf16[192,1536]{1,0:T(8,128)(2,1)}), bf16[768,1536]{1,0:T(8,128)(2,1)}) %all-gather.103.cloned.1.call-update) | async-done | bytes 2359312 | tf_op jit(solution)/shard_map/all_gather | solution.py:349
  1738.3 44.9 %all-gather.123.cloned.1.call-done = bf16[768,1536]{1,0:T(8,128)(2,1)} async-done(((bf16[192,1536]{1,0:T(8,128)(2,1)}), bf16[768,1536]{1,0:T(8,128)(2,1)}) %all-gather.123.cloned.1.call-update) | async-done | bytes 2359312 | tf_op jit(solution)/shard_map/all_gather | solution.py:350
  1787.9 29.4 %all-gather.63.cloned.1.call-done = bf16[768,2304]{1,0:T(8,128)(2,1)} async-done(((bf16[96,2304]{1,0:T(8,128)(2,1)}), bf16[768,2304]{1,0:T(8,128)(2,1)}) %all-gather.63.cloned.1.call-update) | async-done | bytes 3538960 | tf_op jit(solution)/shard_map/all_gather | solution.py:361
  1823.3 20.4 %all-gather.85.cloned.1.call-done = bf16[768,768]{1,0:T(8,128)(2,1)} async-done(((bf16[96,768]{1,0:T(8,128)(2,1)}), bf16[768,768]{1,0:T(8,128)(2,1)}) %all-gather.85.cloned.1.call-update) | async-done | bytes 1179664 | tf_op jit(solution)/shard_map/all_gather | solution.py:368
  1846.6 29.3 %all-gather.105.cloned.1.call-done = bf16[768,768]{1,0:T(8,128)(2,1)} async-done(((bf16[192,768]{1,0:T(8,128)(2,1)}), bf16[768,768]{1,0:T(8,128)(2,1)}) %all-gather.105.cloned.1.call-update) | async-done | bytes 1179664 | tf_op jit(solution)/shard_map/all_gather | solution.py:355
  1879.3 28.3 %all-gather.125.cloned.1.call-done = bf16[768,768]{1,0:T(8,128)(2,1)} async-done(((bf16[192,768]{1,0:T(8,128)(2,1)}), bf16[768,768]{1,0:T(8,128)(2,1)}) %all-gather.125.cloned.1.call-update) | async-done | bytes 1179664 | tf_op jit(solution)/shard_map/all_gather | solution.py:356
  1907.6 4.4 fusion.28
  1912.0 20.5 %all-gather.65.cloned.1.call-done = bf16[768,768]{1,0:T(8,128)(2,1)} async-done(((bf16[96,768]{1,0:T(8,128)(2,1)}), bf16[768,768]{1,0:T(8,128)(2,1)}) %all-gather.65.cloned.1.call-update) | async-done | bytes 1179664 | tf_op jit(solution)/shard_map/all_gather | solution.py:367
  (475 shorter events, 239.4 us)
Async XLA Ops:
  7.2 39.3 %all-gather.43.cloned.1.call-start = ((), (), s32[]{:S(2)}) async-start(), calls=%async_computation.6 | async-start | bytes 3981312 | tf_op jit(solution)/shard_map/all_gather | solution.py:159
  7.9 64.4 %all-gather.45.cloned.1.call-start = ((), (), s32[]{:S(2)}) async-start(), calls=%async_computation.7 | async-start | bytes 1327104 | tf_op jit(solution)/shard_map/all_gather | solution.py:160
  13.4 170.8 %copy-start.81 = (f32[197]{0:T(256)}, f32[197]{0:T(256)S(1)}, u32[]{:S(2)}) copy-start(f32[197]{0:T(256)S(1)} %broadcast_multiply_fusion.6) | copy-start | bytes 2368
  17.5 143.2 %copy-start.76 = (f32[768]{0:T(1024)}, f32[768]{0:T(1024)S(1)}, u32[]{:S(2)}) copy-start(f32[768]{0:T(1024)S(1)} %get-tuple-element.83) | copy-start | bytes 9220
  17.5 166.7 %copy-start.73 = (f32[768]{0:T(1024)}, f32[768]{0:T(1024)S(1)}, u32[]{:S(2)}) copy-start(f32[768]{0:T(1024)S(1)} %get-tuple-element.82) | copy-start | bytes 9220
  74.1 86.6 %copy-start = (f32[197,768]{1,0:T(8,128)}, f32[197,768]{1,0:T(8,128)S(1)}, u32[]{:S(2)}) copy-start(f32[197,768]{1,0:T(8,128)S(1)} %get-tuple-element.77) | copy-start | bytes 1815556
  74.1 86.6 %copy-start.79 = (f32[197]{0:T(256)}, f32[197]{0:T(256)S(1)}, u32[]{:S(2)}) copy-start(f32[197]{0:T(256)S(1)} %broadcast_multiply_fusion.5) | copy-start | bytes 2368
  75.7 11.7 all-to-all-start
  96.7 11.9 all-to-all-start.1
  113.6 11.7 all-to-all-start.2
  130.2 11.7 all-to-all-start.3
  133.6 139.9 %reduce-scatter.3.cloned.1.call-start = ((), (), s32[]{:S(2)}) async-start(), calls=%async_computation.8 | async-start | bytes 10616832 | tf_op jit(solution)/shard_map/reduce_scatter | solution.py:313
  197.6 134.3 %all-reduce.5.cloned.1.call-start = ((), (), s32[]{:S(2)}) async-start(), calls=%async_computation.9 | async-start | bytes 2359296 | tf_op jit(solution)/shard_map/psum | solution.py:329
  273.6 221.1 %reduce-scatter.5.cloned.1.call-start = ((), (), s32[]{:S(2)}) async-start(), calls=%async_computation.10 | async-start | bytes 11796480 | tf_op jit(solution)/shard_map/reduce_scatter | solution.py:255
  280.5 290.7 %all-gather.67.cloned.1.call-start = ((), (), s32[]{:S(2)}) async-start(), calls=%async_computation.21 | async-start | bytes 1327104 | tf_op jit(solution)/shard_map/all_gather | solution.py:362
  334.4 160.3 %copy-start.24 = (f32[1,192,1536]{2,1,0:T(8,128)S(1)}, f32[1,192,1536]{2,1,0:T(8,128)}, u32[]{:S(2)}) copy-start(f32[1,192,1536]{2,1,0:T(8,128)} %param.34) | copy-start | bytes 3538948
  545.9 1275.8 %copy-start.100 = (f32[4,768]{1,0:T(4,128)}, f32[4,768]{1,0:T(4,128)S(1)}, u32[]{:S(2)}) copy-start(f32[4,768]{1,0:T(4,128)S(1)} %get-tuple-element.41) | copy-start | bytes 36868
  549.6 73.7 %all-gather.87.cloned.1.call-start = ((), (), s32[]{:S(2)}) async-start(), calls=%async_computation.31 | async-start | bytes 2949120 | tf_op jit(solution)/shard_map/all_gather | solution.py:349
  555.2 119.0 %all-gather.107.cloned.1.call-start = ((), (), s32[]{:S(2)}) async-start(), calls=%async_computation.41 | async-start | bytes 2949120 | tf_op jit(solution)/shard_map/all_gather | solution.py:350
  556.0 152.8 %all-gather.47.cloned.1.call-start = ((), (), s32[]{:S(2)}) async-start(), calls=%async_computation.11 | async-start | bytes 3981312 | tf_op jit(solution)/shard_map/all_gather | solution.py:361
  557.6 176.9 %all-gather.69.cloned.1.call-start = ((), (), s32[]{:S(2)}) async-start(), calls=%async_computation.22 | async-start | bytes 1327104 | tf_op jit(solution)/shard_map/all_gather | solution.py:368
  573.6 100.6 %copy-start.20 = (bf16[192,1536]{1,0:T(8,128)(2,1)S(1)}, bf16[192,1536]{1,0:T(8,128)(2,1)}, u32[]{:S(2)}) copy-start(bf16[192,1536]{1,0:T(8,128)(2,1)} %get-tuple-element.62) | copy-start | bytes 1769476
  573.6 193.2 %all-gather.89.cloned.1.call-start = ((), (), s32[]{:S(2)}) async-start(), calls=%async_computation.32 | async-start | bytes 1474560 | tf_op jit(solution)/shard_map/all_gather | solution.py:355
  626.6 82.1 %copy-start.17 = (bf16[96,2304]{1,0:T(8,128)(2,1)S(1)}, bf16[96,2304]{1,0:T(8,128)(2,1)}, u32[]{:S(2)}) copy-start(bf16[96,2304]{1,0:T(8,128)(2,1)} %divide_convert_fusion.2) | copy-start | bytes 1327108
  626.6 171.2 %all-gather.109.cloned.1.call-start = ((), (), s32[]{:S(2)}) async-start(), calls=%async_computation.42 | async-start | bytes 1474560 | tf_op jit(solution)/shard_map/all_gather | solution.py:356
  677.6 145.3 %all-gather.49.cloned.1.call-start = ((), (), s32[]{:S(2)}) async-start(), calls=%async_computation.12 | async-start | bytes 1327104 | tf_op jit(solution)/shard_map/all_gather | solution.py:367
  712.7 135.9 %all-gather.71.cloned.1.call-start = ((), (), s32[]{:S(2)}) async-start(), calls=%async_computation.23 | async-start | bytes 1327104 | tf_op jit(solution)/shard_map/all_gather | solution.py:362
  737.0 163.6 %all-gather.91.cloned.1.call-start = ((), (), s32[]{:S(2)}) async-start(), calls=%async_computation.33 | async-start | bytes 2949120 | tf_op jit(solution)/shard_map/all_gather | solution.py:349
  770.6 180.1 %all-gather.111.cloned.1.call-start = ((), (), s32[]{:S(2)}) async-start(), calls=%async_computation.43 | async-start | bytes 2949120 | tf_op jit(solution)/shard_map/all_gather | solution.py:350
  802.0 183.1 %all-gather.51.cloned.1.call-start = ((), (), s32[]{:S(2)}) async-start(), calls=%async_computation.13 | async-start | bytes 3981312 | tf_op jit(solution)/shard_map/all_gather | solution.py:361
  826.1 185.3 %all-gather.73.cloned.1.call-start = ((), (), s32[]{:S(2)}) async-start(), calls=%async_computation.24 | async-start | bytes 1327104 | tf_op jit(solution)/shard_map/all_gather | solution.py:368
  851.1 99.7 %copy-start.45 = (bf16[192,1536]{1,0:T(8,128)(2,1)S(1)}, bf16[192,1536]{1,0:T(8,128)(2,1)}, u32[]{:S(2)}) copy-start(bf16[192,1536]{1,0:T(8,128)(2,1)} %fusion.20) | copy-start | bytes 1769476
  851.1 192.7 %all-gather.93.cloned.1.call-start = ((), (), s32[]{:S(2)}) async-start(), calls=%async_computation.34 | async-start | bytes 1474560 | tf_op jit(solution)/shard_map/all_gather | solution.py:355
  903.9 81.2 %copy-start.14 = (bf16[96,2304]{1,0:T(8,128)(2,1)S(1)}, bf16[96,2304]{1,0:T(8,128)(2,1)}, u32[]{:S(2)}) copy-start(bf16[96,2304]{1,0:T(8,128)(2,1)} %fusion.2) | copy-start | bytes 1327108
  903.9 170.9 %all-gather.113.cloned.1.call-start = ((), (), s32[]{:S(2)}) async-start(), calls=%async_computation.44 | async-start | bytes 1474560 | tf_op jit(solution)/shard_map/all_gather | solution.py:356
  954.1 145.7 %all-gather.53.cloned.1.call-start = ((), (), s32[]{:S(2)}) async-start(), calls=%async_computation.14 | async-start | bytes 1327104 | tf_op jit(solution)/shard_map/all_gather | solution.py:367
  989.1 136.6 %all-gather.75.cloned.1.call-start = ((), (), s32[]{:S(2)}) async-start(), calls=%async_computation.25 | async-start | bytes 1327104 | tf_op jit(solution)/shard_map/all_gather | solution.py:362
  1014.0 163.9 %all-gather.95.cloned.1.call-start = ((), (), s32[]{:S(2)}) async-start(), calls=%async_computation.35 | async-start | bytes 2949120 | tf_op jit(solution)/shard_map/all_gather | solution.py:349
  1047.6 181.0 %all-gather.115.cloned.1.call-start = ((), (), s32[]{:S(2)}) async-start(), calls=%async_computation.45 | async-start | bytes 2949120 | tf_op jit(solution)/shard_map/all_gather | solution.py:350
  1079.0 184.2 %all-gather.55.cloned.1.call-start = ((), (), s32[]{:S(2)}) async-start(), calls=%async_computation.15 | async-start | bytes 3981312 | tf_op jit(solution)/shard_map/all_gather | solution.py:361
  1103.1 185.7 %all-gather.77.cloned.1.call-start = ((), (), s32[]{:S(2)}) async-start(), calls=%async_computation.26 | async-start | bytes 1327104 | tf_op jit(solution)/shard_map/all_gather | solution.py:368
  1128.2 100.4 %copy-start.47 = (bf16[192,1536]{1,0:T(8,128)(2,1)S(1)}, bf16[192,1536]{1,0:T(8,128)(2,1)}, u32[]{:S(2)}) copy-start(bf16[192,1536]{1,0:T(8,128)(2,1)} %fusion.21) | copy-start | bytes 1769476
  1128.2 192.9 %all-gather.97.cloned.1.call-start = ((), (), s32[]{:S(2)}) async-start(), calls=%async_computation.36 | async-start | bytes 1474560 | tf_op jit(solution)/shard_map/all_gather | solution.py:355
  1181.2 82.0 %copy-start.15 = (bf16[96,2304]{1,0:T(8,128)(2,1)S(1)}, bf16[96,2304]{1,0:T(8,128)(2,1)}, u32[]{:S(2)}) copy-start(bf16[96,2304]{1,0:T(8,128)(2,1)} %fusion.3) | copy-start | bytes 1327108
  1181.2 171.0 %all-gather.117.cloned.1.call-start = ((), (), s32[]{:S(2)}) async-start(), calls=%async_computation.46 | async-start | bytes 1474560 | tf_op jit(solution)/shard_map/all_gather | solution.py:356
  1232.0 145.3 %all-gather.57.cloned.1.call-start = ((), (), s32[]{:S(2)}) async-start(), calls=%async_computation.16 | async-start | bytes 1327104 | tf_op jit(solution)/shard_map/all_gather | solution.py:367
  1267.0 135.9 %all-gather.79.cloned.1.call-start = ((), (), s32[]{:S(2)}) async-start(), calls=%async_computation.27 | async-start | bytes 1327104 | tf_op jit(solution)/shard_map/all_gather | solution.py:362
  1291.4 163.7 %all-gather.99.cloned.1.call-start = ((), (), s32[]{:S(2)}) async-start(), calls=%async_computation.37 | async-start | bytes 2949120 | tf_op jit(solution)/shard_map/all_gather | solution.py:349
  1324.9 181.2 %all-gather.119.cloned.1.call-start = ((), (), s32[]{:S(2)}) async-start(), calls=%async_computation.47 | async-start | bytes 2949120 | tf_op jit(solution)/shard_map/all_gather | solution.py:350
  1356.4 184.0 %all-gather.59.cloned.1.call-start = ((), (), s32[]{:S(2)}) async-start(), calls=%async_computation.17 | async-start | bytes 3981312 | tf_op jit(solution)/shard_map/all_gather | solution.py:361
  1380.5 185.7 %all-gather.81.cloned.1.call-start = ((), (), s32[]{:S(2)}) async-start(), calls=%async_computation.28 | async-start | bytes 1327104 | tf_op jit(solution)/shard_map/all_gather | solution.py:368
  1405.5 100.5 %copy-start.49 = (bf16[192,1536]{1,0:T(8,128)(2,1)S(1)}, bf16[192,1536]{1,0:T(8,128)(2,1)}, u32[]{:S(2)}) copy-start(bf16[192,1536]{1,0:T(8,128)(2,1)} %fusion.22) | copy-start | bytes 1769476
  1405.5 193.2 %all-gather.101.cloned.1.call-start = ((), (), s32[]{:S(2)}) async-start(), calls=%async_computation.38 | async-start | bytes 1474560 | tf_op jit(solution)/shard_map/all_gather | solution.py:355
  1458.4 82.0 %copy-start.16 = (bf16[96,2304]{1,0:T(8,128)(2,1)S(1)}, bf16[96,2304]{1,0:T(8,128)(2,1)}, u32[]{:S(2)}) copy-start(bf16[96,2304]{1,0:T(8,128)(2,1)} %fusion.4) | copy-start | bytes 1327108
  1458.4 171.2 %all-gather.121.cloned.1.call-start = ((), (), s32[]{:S(2)}) async-start(), calls=%async_computation.48 | async-start | bytes 1474560 | tf_op jit(solution)/shard_map/all_gather | solution.py:356
  1509.4 145.1 %all-gather.61.cloned.1.call-start = ((), (), s32[]{:S(2)}) async-start(), calls=%async_computation.18 | async-start | bytes 1327104 | tf_op jit(solution)/shard_map/all_gather | solution.py:367
  1544.3 136.1 %all-gather.83.cloned.1.call-start = ((), (), s32[]{:S(2)}) async-start(), calls=%async_computation.29 | async-start | bytes 1327104 | tf_op jit(solution)/shard_map/all_gather | solution.py:362
  1568.8 163.6 %all-gather.103.cloned.1.call-start = ((), (), s32[]{:S(2)}) async-start(), calls=%async_computation.39 | async-start | bytes 2949120 | tf_op jit(solution)/shard_map/all_gather | solution.py:349
  1602.4 180.7 %all-gather.123.cloned.1.call-start = ((), (), s32[]{:S(2)}) async-start(), calls=%async_computation.49 | async-start | bytes 2949120 | tf_op jit(solution)/shard_map/all_gather | solution.py:350
  1633.8 183.4 %all-gather.63.cloned.1.call-start = ((), (), s32[]{:S(2)}) async-start(), calls=%async_computation.19 | async-start | bytes 3981312 | tf_op jit(solution)/shard_map/all_gather | solution.py:361
  1657.8 185.9 %all-gather.85.cloned.1.call-start = ((), (), s32[]{:S(2)}) async-start(), calls=%async_computation.30 | async-start | bytes 1327104 | tf_op jit(solution)/shard_map/all_gather | solution.py:368
  1683.0 193.0 %all-gather.105.cloned.1.call-start = ((), (), s32[]{:S(2)}) async-start(), calls=%async_computation.40 | async-start | bytes 1474560 | tf_op jit(solution)/shard_map/all_gather | solution.py:355
  1735.7 171.9 %all-gather.125.cloned.1.call-start = ((), (), s32[]{:S(2)}) async-start(), calls=%async_computation.50 | async-start | bytes 1474560 | tf_op jit(solution)/shard_map/all_gather | solution.py:356
  1786.5 146.1 %all-gather.65.cloned.1.call-start = ((), (), s32[]{:S(2)}) async-start(), calls=%async_computation.20 | async-start | bytes 1327104 | tf_op jit(solution)/shard_map/all_gather | solution.py:367
  (97 other events, 2825.2 us)
Sparse Core Ops, SparseCore 0:
  9.9 36.5 all-gather.42
  48.4 23.9 all-gather.44
  197.7 75.8 reduce-scatter.2
  275.8 55.9 all-reduce.4
  334.1 160.6 reduce-scatter.4
  549.7 21.4 all-gather.66
  573.3 49.9 all-gather.86
  625.5 48.7 all-gather.106
  676.1 32.5 all-gather.46
  710.5 23.9 all-gather.68
  736.6 30.2 all-gather.88
  768.3 29.4 all-gather.108
  799.7 23.1 all-gather.48
  824.6 23.9 all-gather.70
  850.6 49.9 all-gather.90
  902.0 48.7 all-gather.110
  952.5 32.5 all-gather.50
  987.5 23.9 all-gather.72
  1013.5 30.2 all-gather.92
  1045.3 29.4 all-gather.112
  1076.7 23.1 all-gather.52
  1101.7 23.9 all-gather.74
  1127.8 49.9 all-gather.94
  1179.8 48.7 all-gather.114
  1230.5 32.5 all-gather.54
  1264.9 23.9 all-gather.76
  1290.8 30.2 all-gather.96
  1322.7 29.4 all-gather.116
  1354.1 23.1 all-gather.56
  1379.0 23.9 all-gather.78
  1405.1 49.9 all-gather.98
  1457.3 48.7 all-gather.118
  1507.8 32.5 all-gather.58
  1542.3 23.9 all-gather.80
  1568.4 30.2 all-gather.100
  1600.1 29.4 all-gather.120
  1631.4 23.1 all-gather.60
  1656.4 23.9 all-gather.82
  1682.4 49.9 all-gather.102
  1734.0 49.1 all-gather.122
  1785.0 32.2 all-gather.62
  1819.7 23.9 all-gather.84
  1845.7 30.2 all-gather.104
  1878.1 29.4 all-gather.124
  1909.4 23.1 all-gather.64
where the time goes:
time: 1950 us; the launch traced here: 1940 us
  waiting for transfers between devices  1580 us (81%)
  matrix products  192 us (10%)
  other arithmetic  58.9 us (3%)
  blocking collectives  44.1 us (2%)
  local copies, waits for them, and re-layouts  36.5 us (2%)
  between operations  19.8 us (1%)
    all_gather x5, waiting for transfers between devices, expert_gather(): lax.all_gather(first_rows, 'dp', axis=0, tiled=True)  247 us
    all_gather x5, waiting for transfers between devices, expert_gather(): lax.all_gather(second_rows, 'dp', axis=0, tiled=True)  234 us
    reduce_scatter x1, waiting for transfers between devices, body(): lax.psum_scatter(jnp.concatenate([first_term, second_term], axis=1), 'dp'...  155 us
    all_gather x5, waiting for transfers between devices, attention_gather(): lax.all_gather(first_rows, 'expert', axis=0, tiled=True)  154 us
    all_gather x5, waiting for transfers between devices, expert_grams(): lax.all_gather(first_gram, 'dp', axis=0, tiled=True)  148 us
    all_gather x5, waiting for transfers between devices, expert_grams(): lax.all_gather(second_gram, 'dp', axis=0, tiled=True)  137 us
    all_gather x5, waiting for transfers between devices, attention_grams(): lax.all_gather(second_gram, 'expert', axis=0, tiled=True)  108 us
    all_gather x5, waiting for transfers between devices, attention_grams(): lax.all_gather(first_gram, 'expert', axis=0, tiled=True)  104 us
  transfers between devices with their start and end apart: 49, of which 49 were waited for; matrix products, arithmetic and copies ran while one was open for 10% of the time, Pallas kernels for 0%

commit v1 on v0

--- a/solution.py
+++ b/solution.py
@@ -83,33 +83,26 @@
     return iterate
 
 
-def newton_rows(iter_first, iter_second, gather_pair, gram_pair):
+def ortho_rows(moment, row_start, row_count):
+    norm = jnp.sqrt(jnp.sum(moment * moment)) + frob_eps
+    iterate = (moment / norm).astype(jnp.bfloat16)
     for iteration in range(NS_STEPS):
-        full_first, full_second = gather_pair(iter_first, iter_second)
-        gram_first = lax.dot_general(
-            iter_first, full_first, contract_last, preferred_element_type=jnp.float32
-        ).astype(jnp.bfloat16)
-        gram_second = lax.dot_general(
-            iter_second, full_second, contract_last, preferred_element_type=jnp.float32
-        ).astype(jnp.bfloat16)
-        whole_first, whole_second = gram_pair(gram_first, gram_second)
-        square_first = jnp.dot(gram_first, whole_first, preferred_element_type=jnp.float32)
-        square_second = jnp.dot(gram_second, whole_second, preferred_element_type=jnp.float32)
-        mixer_first = (
-            quintic_two * gram_first.astype(jnp.float32) + quintic_three * square_first
-        ).astype(jnp.bfloat16)
-        mixer_second = (
-            quintic_two * gram_second.astype(jnp.float32) + quintic_three * square_second
-        ).astype(jnp.bfloat16)
-        iter_first = (
-            quintic_one * iter_first.astype(jnp.float32)
-            + jnp.dot(mixer_first, full_first, preferred_element_type=jnp.float32)
-        ).astype(jnp.bfloat16)
-        iter_second = (
-            quintic_one * iter_second.astype(jnp.float32)
-            + jnp.dot(mixer_second, full_second, preferred_element_type=jnp.float32)
-        ).astype(jnp.bfloat16)
-    return (iter_first, iter_second)
+        gram = lax.dot_general(
+            iterate, iterate, contract_last, preferred_element_type=jnp.float32
+        ).astype(jnp.bfloat16)
+        gram_part, iter_part = gram, iterate
+        if iteration == NS_STEPS - 1:
+            gram_part = lax.dynamic_slice_in_dim(gram, row_start, row_count, 0)
+            iter_part = lax.dynamic_slice_in_dim(iterate, row_start, row_count, 0)
+        mixer = (
+            quintic_two * gram_part.astype(jnp.float32)
+            + quintic_three * jnp.dot(gram_part, gram, preferred_element_type=jnp.float32)
+        ).astype(jnp.bfloat16)
+        iterate = (
+            quintic_one * iter_part.astype(jnp.float32)
+            + jnp.dot(mixer, iterate, preferred_element_type=jnp.float32)
+        ).astype(jnp.bfloat16)
+    return iterate
 
 
 def split_heads(qkv_rows, image_count, head_width):
@@ -159,6 +152,9 @@
         lax.all_gather(qkv_weight, "expert", axis=0, tiled=True),
         lax.all_gather(out_weight, "expert", axis=0, tiled=True),
     )
+    moment_pair = jnp.concatenate(
+        [w_in_momentum[0].astype(jnp.bfloat16), w_out_momentum[0].astype(jnp.bfloat16)], axis=1
+    )
     token_float = tokens.astype(jnp.float32)
     scaled_one, inverse_one, normed_one = layer_stats(token_float, ln_gains[0], ln_biases[0])
     attn_in = normed_one.astype(jnp.bfloat16)
@@ -188,6 +184,7 @@
     )
     arrived = lax.all_to_all(dispatch, "expert", split_axis=0, concat_axis=0, tiled=True)
     arrived_rows = arrived.reshape(slots_all, model_width)
+    every_row = lax.all_gather(arrived_rows, "dp", axis=0, tiled=True)
     preact_first = jnp.dot(arrived_rows, first_weight, preferred_element_type=jnp.float32)
     active_first = jax.nn.gelu(preact_first, approximate=False).astype(jnp.bfloat16)
     result = lax.dot_general(
@@ -225,20 +222,14 @@
         .astype(jnp.bfloat16)
         .reshape(experts, capacity, model_width)
     )
-    again_grads, again_rows = (
-        lax.all_to_all(sent_grad, "expert", split_axis=0, concat_axis=0, tiled=True),
-        lax.all_to_all(dispatch, "expert", split_axis=0, concat_axis=0, tiled=True),
-    )
+    again_grads = lax.all_to_all(sent_grad, "expert", split_axis=0, concat_axis=0, tiled=True)
     grad_rows = again_grads.reshape(slots_all, model_width)
-    rows_used = again_rows.reshape(slots_all, model_width)
-    preact_again = jnp.dot(rows_used, first_weight, preferred_element_type=jnp.float32)
-    active = jax.nn.gelu(preact_again, approximate=False).astype(jnp.bfloat16)
+    every_grad = lax.all_gather(grad_rows, "dp", axis=0, tiled=True)
     act_grad = jnp.dot(grad_rows, second_weight, preferred_element_type=jnp.float32)
-    expert_pre_grad = (act_grad * gelu_slope(preact_again)).astype(jnp.bfloat16)
+    expert_pre_grad = (act_grad * gelu_slope(preact_first)).astype(jnp.bfloat16)
     row_grad = lax.dot_general(
         expert_pre_grad, first_weight, contract_last, preferred_element_type=jnp.float32
     ).astype(jnp.bfloat16)
-    pre_grad, row_grad = (expert_pre_grad, row_grad)
     returned_grad = lax.all_to_all(
         row_grad.reshape(experts, capacity, model_width),
         "expert",
@@ -246,17 +237,6 @@
         concat_axis=0,
         tiled=True,
     )
-    first_term = lax.dot_general(
-        rows_used, pre_grad, contract_first, preferred_element_type=jnp.float32
-    )
-    second_term = lax.dot_general(
-        grad_rows, active, contract_first, preferred_element_type=jnp.float32
-    )
-    summed = lax.psum_scatter(
-        jnp.concatenate([first_term, second_term], axis=1), "dp", scatter_dimension=0, tiled=True
-    )
-    grad_first = summed[:, :hidden_units]
-    grad_second = summed[:, hidden_units:]
     gathered = (
         jnp.take(
             returned_grad.reshape(slots_all, model_width),
@@ -311,7 +291,10 @@
         mixed_rows, middle_rounded, contract_first, preferred_element_type=jnp.float32
     )
     attention_share = lax.psum_scatter(
-        jnp.concatenate([qkv_term, out_term], axis=1), "expert", scatter_dimension=0, tiled=True
+        jnp.concatenate([qkv_term, out_term], axis=1).astype(jnp.bfloat16),
+        "expert",
+        scatter_dimension=0,
+        tiled=True,
     )
     norm_local = jnp.stack(
         [
@@ -321,60 +304,54 @@
             jnp.sum(normed_grad, axis=0),
         ]
     )
-    moment_first = decay_rate * w_in_momentum[0] + grad_first
-    moment_second = decay_rate * w_out_momentum[0] + grad_second
-    expert_squares = jnp.stack(
-        [jnp.sum(moment_first * moment_first), jnp.sum(moment_second * moment_second)]
-    )
-    attention_total, squares_total, router_part, norm_part = lax.psum(
-        (attention_share, expert_squares, router_local, norm_local), "dp"
-    )
+    attention_total = lax.psum(attention_share, "dp").astype(jnp.float32)
+    small_parts = lax.all_gather(
+        jnp.concatenate([router_local.T, norm_local], axis=0), ("dp", "expert"), axis=0
+    )
+    small_total = jnp.sum(small_parts, axis=0)
+    grad_router = small_total[:experts].T
+    grad_norm = small_total[experts:]
     grad_qkv = attention_total[:, : 3 * model_width]
     grad_out = attention_total[:, 3 * model_width :]
     moment_qkv = decay_rate * qkv_momentum + grad_qkv
     moment_out = decay_rate * out_momentum + grad_out
-    attention_squares = jnp.stack(
-        [jnp.sum(moment_qkv * moment_qkv), jnp.sum(moment_out * moment_out)]
-    )
-    grad_router, grad_norm, attention_norms = lax.psum(
-        (router_part, norm_part, attention_squares), "expert"
-    )
+    whole_qkv = lax.all_gather(moment_qkv.astype(jnp.bfloat16), "expert", axis=0, tiled=True)
+    whole_out = lax.all_gather(moment_out.astype(jnp.bfloat16), "expert", axis=0, tiled=True)
+    row_base = lax.axis_index("dp") * dp_share
+    every_moment = lax.all_gather(moment_pair, "dp", axis=0, tiled=True)
+    every_preact = jnp.dot(every_row, first_weight, preferred_element_type=jnp.float32)
+    every_active = jax.nn.gelu(every_preact, approximate=False).astype(jnp.bfloat16)
+    every_act_grad = jnp.dot(every_grad, second_weight, preferred_element_type=jnp.float32)
+    every_pre_grad = (every_act_grad * gelu_slope(every_preact)).astype(jnp.bfloat16)
+    whole_first = lax.dot_general(
+        every_row, every_pre_grad, contract_first, preferred_element_type=jnp.float32
+    )
+    whole_second = lax.dot_general(
+        every_grad, every_active, contract_first, preferred_element_type=jnp.float32
+    )
+    grad_first = lax.dynamic_slice_in_dim(whole_first, row_base, dp_share, 0)
+    grad_second = lax.dynamic_slice_in_dim(whole_second, row_base, dp_share, 0)
+    moment_first = decay_rate * w_in_momentum[0] + grad_first
+    moment_second = decay_rate * w_out_momentum[0] + grad_second
+    iter_first = ortho_rows(
+        decay_rate * every_moment[:, :hidden_units].astype(jnp.float32) + whole_first,
+        row_base,
+        dp_share,
+    )
+    iter_second = ortho_rows(
+        decay_rate * every_moment[:, hidden_units:].astype(jnp.float32) + whole_second,
+        row_base,
+        dp_share,
+    )
+    expert_share = qkv_weight.shape[0]
+    expert_base = lax.axis_index("expert") * expert_share
+    iter_out = ortho_rows(whole_out.astype(jnp.float32), expert_base, expert_share)
+    iter_qkv = ortho_rows(whole_qkv.astype(jnp.float32), expert_base, expert_share)
     new_norm_momentum = decay_rate * norm_momentum + grad_norm
     new_norm = jnp.concatenate([ln_gains, ln_biases], axis=0) - norm_rate * new_norm_momentum
     new_router_momentum = decay_rate * router_momentum + grad_router
     new_router = router - matrix_rate * ortho_tall(new_router_momentum).astype(jnp.float32)
 
-    def expert_gather(first_rows, second_rows):
-        return (
-            lax.all_gather(first_rows, "dp", axis=0, tiled=True),
-            lax.all_gather(second_rows, "dp", axis=0, tiled=True),
-        )
-
-    def expert_grams(first_gram, second_gram):
-        return (
-            lax.all_gather(first_gram, "dp", axis=0, tiled=True),
-            lax.all_gather(second_gram, "dp", axis=0, tiled=True),
-        )
-
-    def attention_gather(first_rows, second_rows):
-        return (
-            lax.all_gather(first_rows, "expert", axis=0, tiled=True),
-            lax.all_gather(second_rows, "expert", axis=0, tiled=True),
-        )
-
-    def attention_grams(first_gram, second_gram):
-        return (
-            lax.all_gather(first_gram, "expert", axis=0, tiled=True),
-            lax.all_gather(second_gram, "expert", axis=0, tiled=True),
-        )
-
-    iter_first = (moment_first / (jnp.sqrt(squares_total[0]) + frob_eps)).astype(jnp.bfloat16)
-    iter_second = (moment_second / (jnp.sqrt(squares_total[1]) + frob_eps)).astype(jnp.bfloat16)
-    iter_first, iter_second = newton_rows(iter_first, iter_second, expert_gather, expert_grams)
-    iter_qkv = (moment_qkv / (jnp.sqrt(attention_norms[0]) + frob_eps)).astype(jnp.bfloat16)
-    iter_out = (moment_out / (jnp.sqrt(attention_norms[1]) + frob_eps)).astype(jnp.bfloat16)
-    iter_qkv, iter_out = newton_rows(iter_qkv, iter_out, attention_gather, attention_grams)
-    row_base = lax.axis_index("dp") * dp_share
     rows_first = lax.dynamic_slice_in_dim(first_weight, row_base, dp_share, 0).astype(jnp.float32)
     rows_second = lax.dynamic_slice_in_dim(second_weight, row_base, dp_share, 0).astype(jnp.float32)
     widen_factor = math.sqrt(max(1.0, hidden_units / model_width))

time: 1950 us -> 562 us (0.29)
  waiting for transfers between devices: 1580 us -> 158 us
  matrix products: 192 us -> 268 us
  blocking collectives: 44.1 us -> 10.7 us
    all_gather x40 -> x6, waiting for transfers between devices: 1240 us -> 68.1 us  [the longest x1 35.3 us: body(): every_moment = lax.all_gather(moment_pair, 'dp', axis=0, tiled=True)]
    reduce_scatter x2 -> x1, waiting for transfers between devices: 231 us -> 0.01 us  [body(): lax.psum_scatter(jnp.concatenate([qkv_term, out_term], axis=1).astype(jnp...]
    dot_general x43, matrix products: 138 us -> 219 us  [the longest x20 105 us: ortho_rows(): jnp.dot(mixer, iterate, preferred_element_type=jnp.float32)]
    psum x2 -> x0, blocking collectives: 44.1 us -> none  [the longest x1 23.8 us: body(): lax.psum((router_part, norm_part, attention_squares), 'expert')]
  transfers between devices with their start and end apart: 49 -> 13, of which waited for: 49 -> 9; matrix products, arithmetic and copies ran while one was open for 10% -> 50% of each run, Pallas kernels for 0% -> 0%
where the time goes in v1:
time: 562 us; the launch traced here: 553 us
  matrix products  268 us (48%)
  waiting for transfers between devices  158 us (28%)
  other arithmetic  53.7 us (10%)
  local copies, waits for them, and re-layouts  32.5 us (6%)
  between operations  18.9 us (3%)
  starting transfers between devices  11.3 us (2%)
  blocking collectives  10.7 us (2%)
    dot_general x20, matrix products, ortho_rows(): jnp.dot(mixer, iterate, preferred_element_type=jnp.float32)  105 us
    dot_general x20, matrix products, ortho_rows(): lax.dot_general(iterate, iterate, contract_last, preferred_element_type=j...  79.2 us
    all_gather x1, waiting for transfers between devices, body(): every_moment = lax.all_gather(moment_pair, 'dp', axis=0, tiled=True)  35.3 us
    psum x1, waiting for transfers between devices, body(): attention_total = lax.psum(attention_share, 'dp').astype(jnp.float32)  30 us
    all_gather x1, waiting for transfers between devices, body(): lax.all_gather(qkv_weight, 'expert', axis=0, tiled=True)  28.4 us
    dot_general x1, matrix products, body(): lax.dot_general(every_grad, every_active, contract_first, preferred_eleme...  18.2 us
    all_gather x1, waiting for transfers between devices, body(): lax.all_gather(moment_out.astype(jnp.bfloat16), 'expert', axis=0, tiled=T...  17.2 us
    all_gather x1, waiting for transfers between devices, body(): lax.all_gather(out_weight, 'expert', axis=0, tiled=True)  16.8 us
  transfers between devices with their start and end apart: 13, of which 9 were waited for; matrix products, arithmetic and copies ran while one was open for 50% of the time, Pallas kernels for 0%

profile of v1, /device:TPU:0, one launch (start us, length us, event | category | flops | bytes accessed | tf_op | source)
XLA Modules:
  0.0 552.9 jit_solution(16380432145679029970)
XLA Ops:
  18.1 28.4 %all-gather.11.cloned.1.call-done = bf16[768,2304]{1,0:T(8,128)(2,1)} async-done(((bf16[96,2304]{1,0:T(8,128)(2,1)}), bf16[768,2304]{1,0:T(8,128)(2,1)}) %all-gather.11.cloned.1.call-update) | async-done | bytes 3538960 | tf_op jit(solution)/shard_map/all_gather | solution.py:152
  46.5 3.0 convolution_convert_fusion.1
  52.1 3.4 convolution_convert_fusion.24
  55.5 16.8 %all-gather.13.cloned.1.call-done = bf16[768,768]{1,0:T(8,128)(2,1)} async-done(((bf16[96,768]{1,0:T(8,128)(2,1)}), bf16[768,768]{1,0:T(8,128)(2,1)}) %all-gather.13.cloned.1.call-update) | async-done | bytes 1179664 | tf_op jit(solution)/shard_map/all_gather | solution.py:153
  75.7 3.5 all-to-all-start
  84.0 3.4 all-to-all-done
  88.3 2.5 fusion.52
  91.9 3.2 fusion.84
  96.0 3.5 all-to-all-start.1
  100.4 4.6 gather_fusion.1
  113.9 10.7 %all_to_all.20 = bf16[8,25,768]{2,1,0:T(8,128)(2,1)S(1)} all-to-all(bf16[8,25,768]{2,1,0:T(8,128)(2,1)S(1)} %reshape.327), channel_id=1, replica_groups=mesh['dp'=4,'expert'=8] {'expert'}, dimensions={0} | all-to-all | bytes 614400 | tf_op jit(solution)/shard_map/all_to_all | solution.py:225
  128.2 4.3 fusion.38
  132.5 4.0 fusion.81
  137.4 3.5 all-to-all-start.3
  141.0 8.1 %all-to-all-done.3 = bf16[8,25,768]{2,1,0:T(8,128)(2,1)S(1)} async-done(((bf16[8,25,768]{2,1,0:T(8,128)(2,1)}), bf16[8,25,768]{2,1,0:T(8,128)(2,1)S(1)}, u32[]{:S(2)}, u32[]{:S(2)}) %all-to-all-start.3) | async-done | bytes 307232 | tf_op jit(solution)/shard_map/all_to_all | solution.py:233
  152.7 3.1 reshape.336
  157.6 2.8 reduce_sum.225
  165.3 3.9 fusion.89
  171.2 4.8 fusion.90
  176.0 4.9 fusion.91
  184.1 2.8 pad_maximum_fusion
  188.4 3.5 fusion.138
  194.3 6.5 %fusion.48 = f32[800,1536]{1,0:T(8,128)} fusion(bf16[800,768]{1,0:T(8,128)(2,1)} %all-gather.15.cloned.1.call-done, bf16[1,768,1536]{2,1,0:T(8,128)(2,1)} %param.28), kind=kOutput, calls=%fused_computation.95 | convolution fusion | flops 1887436800 | bytes 8503296 | tf_op jit(solution)/shard_map/dot_general | solution.py:322
  200.8 10.3 %fusion.129 = f32[768,1536]{1,0:T(8,128)} fusion(bf16[800,768]{1,0:T(8,128)(2,1)} %all-gather.15.cloned.1.call-done, f32[800,1536]{1,0:T(8,128)} %fusion.48, bf16[800,768]{1,0:T(8,128)(2,1)} %all-gather.17.cloned.1.call-done, bf16[1,768,1536]{2,1,0:T(8,128)(2,1)S(1)} %copy-done.57), kind=kOutput, calls=%fused_computation.256 | convolution fusion | flops 3787161600 | bytes 14450688 | tf_op jit(solution)/shard_map/dot_general | solution.py:326
  211.1 35.3 %all-gather.23.cloned.1.call-done = bf16[768,3072]{1,0:T(8,128)(2,1)} async-done(((bf16[192,3072]{1,0:T(8,128)(2,1)}), bf16[768,3072]{1,0:T(8,128)(2,1)}) %all-gather.23.cloned.1.call-update) | async-done | bytes 4718608 | tf_op jit(solution)/shard_map/all_gather | solution.py:321
  246.4 18.2 %multiply_reduce_fusion = (f32[]{:T(128)}, f32[]{:T(128)}, f32[768,1536]{1,0:T(8,128)}) fusion(bf16[768,3072]{1,0:T(8,128)(2,1)} %all-gather.23.cloned.1.call-done, f32[768,1536]{1,0:T(8,128)} %fusion.129, bf16[800,768]{1,0:T(8,128)(2,1)} %all-gather.17.cloned.1.call-done, f32[800,1536]{1,0:T(8,128)} %fusion.48), kind=kOutput, calls=%fused_computation.48 | convolution fusion | flops 1979105280 | bytes 20299784 | tf_op jit(solution)/shard_map/dot_general | solution.py:329
  266.0 6.3 %divide_convert_fusion = (bf16[768,1536]{1,0:T(8,128)(2,1)S(1)}, bf16[768,1536]{1,0:T(8,128)(2,1)S(1)}) fusion(f32[768,1536]{1,0:T(8,128)} %get-tuple-element.72, f32[]{:T(128)S(6)} %add.415, bf16[768,3072]{1,0:T(8,128)(2,1)} %all-gather.23.cloned.1.call-done, f32[]{:T(128)S(6)} %add.402, f32[768,1536]{1,0:T(8,128)} %fusion.129), kind=kLoop, calls=%fused_computation.47 | loop fusion | flops 11796480 | bytes 18874376 | tf_op jit(solution)/shard_map/convert_element_type | solution.py:88
  275.7 6.6 %add_convert_fusion.7 = bf16[768,1536]{1,0:T(8,128)(2,1)} fusion(bf16[768,1536]{1,0:T(8,128)(2,1)} %copy-done.9, bf16[768,768]{1,0:T(8,128)(2,1)S(1)} %convolution_convert_fusion.17), kind=kOutput, calls=%fused_computation.46 | convolution fusion | flops 2725576704 | bytes 5898240 | tf_op jit(solution)/shard_map/dot_general | solution.py:103
  282.4 4.5 convolution_convert_fusion.16
  286.9 6.5 %add_convert_fusion.6 = bf16[768,1536]{1,0:T(8,128)(2,1)} fusion(bf16[768,1536]{1,0:T(8,128)(2,1)} %add_convert_fusion.7, bf16[768,768]{1,0:T(8,128)(2,1)S(1)} %convolution_convert_fusion.16), kind=kOutput, calls=%fused_computation.45 | convolution fusion | flops 2725576704 | bytes 5898240 | tf_op jit(solution)/shard_map/dot_general | solution.py:103
  293.3 4.4 convolution_convert_fusion.15
  297.8 6.7 %add_convert_fusion.5 = bf16[768,1536]{1,0:T(8,128)(2,1)} fusion(bf16[768,1536]{1,0:T(8,128)(2,1)} %add_convert_fusion.6, bf16[768,768]{1,0:T(8,128)(2,1)S(1)} %convolution_convert_fusion.15), kind=kOutput, calls=%fused_computation.44 | convolution fusion | flops 2725576704 | bytes 5898240 | tf_op jit(solution)/shard_map/dot_general | solution.py:103
  304.4 4.4 convolution_convert_fusion.14
  308.8 6.9 %add_convert_fusion.4 = bf16[768,1536]{1,0:T(8,128)(2,1)} fusion(bf16[768,1536]{1,0:T(8,128)(2,1)} %add_convert_fusion.5, bf16[768,768]{1,0:T(8,128)(2,1)S(1)} %convolution_convert_fusion.14), kind=kOutput, calls=%fused_computation.43 | convolution fusion | flops 2725576704 | bytes 5898240 | tf_op jit(solution)/shard_map/dot_general | solution.py:103
  315.7 4.4 convolution_convert_fusion.13
  320.1 3.0 convolution_convert_fusion.22
  323.2 6.5 %add_convert_fusion.11 = bf16[768,1536]{1,0:T(8,128)(2,1)} fusion(bf16[768,1536]{1,0:T(8,128)(2,1)S(1)} %get-tuple-element.57, bf16[768,768]{1,0:T(8,128)(2,1)} %convolution_convert_fusion.22), kind=kOutput, calls=%fused_computation.53 | convolution fusion | flops 2725576704 | bytes 5898240 | tf_op jit(solution)/shard_map/dot_general | solution.py:103
  329.7 5.6 %convolution_convert_fusion.21 = bf16[768,768]{1,0:T(8,128)(2,1)} fusion(bf16[768,1536]{1,0:T(8,128)(2,1)} %add_convert_fusion.11), kind=kOutput, calls=%fused_computation.146 | convolution fusion | flops 1812529152 | bytes 3538944 | tf_op jit(solution)/shard_map/dot_general | solution.py:90
  335.3 6.5 %add_convert_fusion.10 = bf16[768,1536]{1,0:T(8,128)(2,1)} fusion(bf16[768,1536]{1,0:T(8,128)(2,1)S(1)} %copy-done.59, bf16[768,768]{1,0:T(8,128)(2,1)} %convolution_convert_fusion.21), kind=kOutput, calls=%fused_computation.52 | convolution fusion | flops 2725576704 | bytes 5898240 | tf_op jit(solution)/shard_map/dot_general | solution.py:103
  341.8 5.6 %convolution_convert_fusion.20 = bf16[768,768]{1,0:T(8,128)(2,1)} fusion(bf16[768,1536]{1,0:T(8,128)(2,1)} %add_convert_fusion.10), kind=kOutput, calls=%fused_computation.145 | convolution fusion | flops 1812529152 | bytes 3538944 | tf_op jit(solution)/shard_map/dot_general | solution.py:90
  347.4 6.5 %add_convert_fusion.9 = bf16[768,1536]{1,0:T(8,128)(2,1)} fusion(bf16[768,1536]{1,0:T(8,128)(2,1)S(1)} %copy-done.60, bf16[768,768]{1,0:T(8,128)(2,1)} %convolution_convert_fusion.20), kind=kOutput, calls=%fused_computation.51 | convolution fusion | flops 2725576704 | bytes 5898240 | tf_op jit(solution)/shard_map/dot_general | solution.py:103
  353.9 5.6 %convolution_convert_fusion.19 = bf16[768,768]{1,0:T(8,128)(2,1)} fusion(bf16[768,1536]{1,0:T(8,128)(2,1)} %add_convert_fusion.9), kind=kOutput, calls=%fused_computation.144 | convolution fusion | flops 1812529152 | bytes 3538944 | tf_op jit(solution)/shard_map/dot_general | solution.py:90
  359.5 3.0 fusion.34
  362.5 6.9 %add_convert_fusion.8 = bf16[768,1536]{1,0:T(8,128)(2,1)S(1)} fusion(bf16[768,1536]{1,0:T(8,128)(2,1)} %add_convert_fusion.9, bf16[768,768]{1,0:T(8,128)(2,1)} %convolution_convert_fusion.19), kind=kOutput, calls=%fused_computation.50 | convolution fusion | flops 2725576704 | bytes 5898240 | tf_op jit(solution)/shard_map/dot_general | solution.py:103
  369.4 3.0 convolution_convert_fusion.18
  372.5 2.8 fusion.93
  375.4 3.7 fusion.29
  379.1 2.9 fusion.92
  383.6 30.0 %all-reduce.3.cloned.1.call-done = bf16[96,3072]{1,0:T(8,128)(2,1)} async-done(((bf16[96,3072]{1,0:T(8,128)(2,1)}), bf16[96,3072]{1,0:T(8,128)(2,1)}) %all-reduce.3.cloned.1.call-update) | async-done | bytes 589840 | tf_op jit(solution)/shard_map/psum | solution.py:307
  422.5 17.2 %all-gather.21.cloned.1.call-done = bf16[768,768]{1,0:T(8,128)(2,1)} async-done(((bf16[96,768]{1,0:T(8,128)(2,1)}), bf16[768,768]{1,0:T(8,128)(2,1)}) %all-gather.21.cloned.1.call-update) | async-done | bytes 1179664 | tf_op jit(solution)/shard_map/all_gather | solution.py:319
  439.7 2.5 fusion.42
  442.9 2.9 convolution_convert_fusion.11
  460.3 15.6 %all-gather.19.cloned.1.call-done = bf16[768,2304]{1,0:T(8,128)(2,1)} async-done(((bf16[96,2304]{1,0:T(8,128)(2,1)}), bf16[768,2304]{1,0:T(8,128)(2,1)}) %all-gather.19.cloned.1.call-update) | async-done | bytes 3538960 | tf_op jit(solution)/shard_map/all_gather | solution.py:318
  475.8 5.0 fusion.2
  481.5 4.0 convolution_convert_fusion.6
  485.5 7.8 %add_convert_fusion.3 = bf16[768,2304]{1,0:T(8,128)(2,1)} fusion(bf16[768,768]{1,0:T(8,128)(2,1)} %convolution_convert_fusion.6, f32[]{:T(128)S(6)} %add.377, bf16[768,2304]{1,0:T(8,128)(2,1)S(1)} %copy-done.8), kind=kOutput, calls=%fused_computation.16 | convolution fusion | flops 3644522496 | bytes 8257540 | tf_op jit(solution)/shard_map/dot_general | solution.py:103
  493.3 7.1 %convolution_convert_fusion.5 = bf16[768,768]{1,0:T(8,128)(2,1)} fusion(bf16[768,2304]{1,0:T(8,128)(2,1)} %add_convert_fusion.3), kind=kOutput, calls=%fused_computation.130 | convolution fusion | flops 2718498816 | bytes 4718592 | tf_op jit(solution)/shard_map/dot_general | solution.py:90
  500.5 7.8 %add_convert_fusion.2 = bf16[768,2304]{1,0:T(8,128)(2,1)} fusion(bf16[768,2304]{1,0:T(8,128)(2,1)S(1)} %copy-done.61, bf16[768,768]{1,0:T(8,128)(2,1)} %convolution_convert_fusion.5), kind=kOutput, calls=%fused_computation.15 | convolution fusion | flops 3633905664 | bytes 8257536 | tf_op jit(solution)/shard_map/dot_general | solution.py:103
  508.3 7.3 %convolution_convert_fusion.4 = bf16[768,768]{1,0:T(8,128)(2,1)} fusion(bf16[768,2304]{1,0:T(8,128)(2,1)} %add_convert_fusion.2), kind=kOutput, calls=%fused_computation.129 | convolution fusion | flops 2718498816 | bytes 4718592 | tf_op jit(solution)/shard_map/dot_general | solution.py:90
  515.6 7.8 %add_convert_fusion.1 = bf16[768,2304]{1,0:T(8,128)(2,1)} fusion(bf16[768,2304]{1,0:T(8,128)(2,1)S(1)} %copy-done.62, bf16[768,768]{1,0:T(8,128)(2,1)} %convolution_convert_fusion.4), kind=kOutput, calls=%fused_computation.14 | convolution fusion | flops 3633905664 | bytes 8257536 | tf_op jit(solution)/shard_map/dot_general | solution.py:103
  523.4 7.0 %convolution_convert_fusion.3 = bf16[768,768]{1,0:T(8,128)(2,1)} fusion(bf16[768,2304]{1,0:T(8,128)(2,1)} %add_convert_fusion.1), kind=kOutput, calls=%fused_computation.128 | convolution fusion | flops 2718498816 | bytes 4718592 | tf_op jit(solution)/shard_map/dot_general | solution.py:90
  530.4 8.1 %add_convert_fusion = bf16[768,2304]{1,0:T(8,128)(2,1)S(1)} fusion(bf16[768,2304]{1,0:T(8,128)(2,1)} %add_convert_fusion.1, bf16[768,768]{1,0:T(8,128)(2,1)} %convolution_convert_fusion.3), kind=kOutput, calls=%fused_computation.13 | convolution fusion | flops 3633905664 | bytes 8257536 | tf_op jit(solution)/shard_map/dot_general | solution.py:103
  538.5 3.9 convolution_convert_fusion.2
  542.5 3.4 fusion.23
  (268 shorter events, 85.2 us)
Async XLA Ops:
  7.2 9.3 %copy-start.29 = (f32[2,768]{1,0:T(2,128)S(1)}, f32[2,768]{1,0:T(2,128)}, u32[]{:S(2)}) copy-start(f32[2,768]{1,0:T(2,128)} %param.24) | copy-start | bytes 18436
  7.2 9.3 %copy-start.31 = (f32[2,768]{1,0:T(2,128)S(1)}, f32[2,768]{1,0:T(2,128)}, u32[]{:S(2)}) copy-start(f32[2,768]{1,0:T(2,128)} %param.23) | copy-start | bytes 18436
  7.2 9.8 %copy-start = (bf16[197,768]{1,0:T(8,128)(2,1)S(1)}, bf16[197,768]{1,0:T(8,128)(2,1)}, u32[]{:S(2)}) copy-start(bf16[197,768]{1,0:T(8,128)(2,1)} %param.19) | copy-start | bytes 907780
  7.2 39.3 %all-gather.11.cloned.1.call-start = ((), (), s32[]{:S(2)}) async-start(), calls=%async_computation.5 | async-start | bytes 3981312 | tf_op jit(solution)/shard_map/all_gather | solution.py:152
  8.0 64.4 %all-gather.13.cloned.1.call-start = ((), (), s32[]{:S(2)}) async-start(), calls=%async_computation.6 | async-start | bytes 1327104 | tf_op jit(solution)/shard_map/all_gather | solution.py:153
  16.5 58.0 %copy-start.52 = (s32[197]{0:T(256)}, s32[197]{0:T(256)S(1)}, u32[]{:S(2)}) copy-start(s32[197]{0:T(256)S(1)} %get-tuple-element.33) | copy-start | bytes 2368
  16.5 58.0 %copy-start.54 = (s32[197]{0:T(256)}, s32[197]{0:T(256)S(1)}, u32[]{:S(2)}) copy-start(s32[197]{0:T(256)S(1)} %get-tuple-element.34) | copy-start | bytes 2368
  16.6 57.9 %copy-start.39 = (f32[768]{0:T(1024)}, f32[768]{0:T(1024)S(1)}, u32[]{:S(2)}) copy-start(f32[768]{0:T(1024)S(1)} %get-tuple-element.39) | copy-start | bytes 9220
  17.4 32.1 %copy-start.37 = (f32[197]{0:T(256)}, f32[197]{0:T(256)S(1)}, u32[]{:S(2)}) copy-start(f32[197]{0:T(256)S(1)} %add_rsqrt_fusion.1) | copy-start | bytes 2368
  50.1 5.4 copy-start.6
  55.5 20.2 %copy-start.13 = (bf16[12,64,197]{2,1,0:T(8,128)(2,1)}, bf16[12,64,197]{2,1,0:T(8,128)(2,1)S(1)}, u32[]{:S(2)}) copy-start(bf16[12,64,197]{2,1,0:T(8,128)(2,1)S(1)} %convolution_convert_fusion.24) | copy-start | bytes 907780
  72.3 7.5 %copy-start.23 = (s32[197,2,1]{1,0,2:T(8,128)S(1)}, s32[197,2,1]{1,0,2:T(8,128)}, u32[]{:S(2)}) copy-start(s32[197,2,1]{1,0,2:T(8,128)} %bitcast_or_fusion) | copy-start | bytes 4732
  72.3 7.7 %copy-start.15 = (bf16[197,768]{1,0:T(8,128)(2,1)S(1)}, bf16[197,768]{1,0:T(8,128)(2,1)}, u32[]{:S(2)}) copy-start(bf16[197,768]{1,0:T(8,128)(2,1)} %param.20) | copy-start | bytes 907780
  74.4 25.3 %copy-start.35 = (f32[197]{0:T(256)}, f32[197]{0:T(256)S(1)}, u32[]{:S(2)}) copy-start(f32[197]{0:T(256)S(1)} %add_rsqrt_fusion) | copy-start | bytes 2368
  75.7 11.7 %all-to-all-start = ((bf16[8,25,768]{2,1,0:T(8,128)(2,1)}), bf16[8,25,768]{2,1,0:T(8,128)(2,1)S(1)}, u32[]{:S(2)}, u32[]{:S(2)}) async-start(bf16[8,25,768]{2,1,0:T(8,128)(2,1)} %reshape.322), calls=%async_computation | async-start | bytes 786432 | tf_op jit(solution)/shard_map/all_to_all | solution.py:185
  79.2 115.1 %all-gather.15.cloned.1.call-start = ((), (), s32[]{:S(2)}) async-start(), calls=%async_computation.9 | async-start | bytes 1536000 | tf_op jit(solution)/shard_map/all_gather | solution.py:187
  88.3 3.6 copy-start.56
  91.9 7.8 %copy-start.25 = (f32[768,8]{0,1:T(8,128)S(1)}, f32[768,8]{0,1:T(8,128)}, u32[]{:S(2)}) copy-start(f32[768,8]{0,1:T(8,128)} %param.27) | copy-start | bytes 73732
  91.9 7.8 %copy-start.40 = (f32[768]{0:T(1024)S(1)}, f32[768]{0:T(1024)}, u32[]{:S(2)}) copy-start(f32[768]{0:T(1024)} %copy-done.39) | copy-start | bytes 9220
  96.0 11.7 %all-to-all-start.1 = ((bf16[8,25,768]{2,1,0:T(8,128)(2,1)}), bf16[8,25,768]{2,1,0:T(8,128)(2,1)S(1)}, u32[]{:S(2)}, u32[]{:S(2)}) async-start(bf16[8,25,768]{2,1,0:T(8,128)(2,1)} %reshape.324), calls=%async_computation.1 | async-start | bytes 786432 | tf_op jit(solution)/shard_map/all_to_all | solution.py:193
  99.5 101.3 %all-gather.17.cloned.1.call-start = ((), (), s32[]{:S(2)}) async-start(), calls=%async_computation.10 | async-start | bytes 1536000 | tf_op jit(solution)/shard_map/all_gather | solution.py:227
  107.9 2.5 copy-start.45
  107.9 3.0 copy-start.20
  110.7 14.8 %copy-start.2 = (f32[1,192,1536]{2,1,0:T(8,128)S(1)}, f32[1,192,1536]{2,1,0:T(8,128)}, u32[]{:S(2)}) copy-start(f32[1,192,1536]{2,1,0:T(8,128)} %param.34) | copy-start | bytes 3538948
  111.6 50.3 %copy-start.46 = (f32[197]{0:T(256)}, f32[197]{0:T(256)S(1)}, u32[]{:S(2)}) copy-start(f32[197]{0:T(256)S(1)} %get-tuple-element.31) | copy-start | bytes 2368
  125.5 120.9 %all-gather.23.cloned.1.call-start = ((), (), s32[]{:S(2)}) async-start(), calls=%async_computation.13 | async-start | bytes 5898240 | tf_op jit(solution)/shard_map/all_gather | solution.py:321
  128.1 4.4 copy-start.12
  128.1 4.4 copy-start.17
  128.2 33.8 %copy-start.48 = (s32[197,1]{0,1:T(1,128)}, s32[197,1]{0,1:T(1,128)S(1)}, u32[]{:S(2)}) copy-start(s32[197,1]{0,1:T(1,128)S(1)} %get-tuple-element.62) | copy-start | bytes 2368
  128.2 33.8 %copy-start.50 = (s32[197,1]{0,1:T(1,128)}, s32[197,1]{0,1:T(1,128)S(1)}, u32[]{:S(2)}) copy-start(s32[197,1]{0,1:T(1,128)S(1)} %get-tuple-element.63) | copy-start | bytes 2368
  132.5 8.4 %copy-start.19 = (f32[197,1]{1,0:T(8,128)S(1)}, f32[197,1]{1,0:T(8,128)}, u32[]{:S(2)}) copy-start(f32[197,1]{1,0:T(8,128)} %get-tuple-element.53) | copy-start | bytes 2368
  136.5 12.7 %copy-start.34 = (s32[1024]{0:T(1024)S(1)}, s32[1024]{0:T(1024)}, u32[]{:S(2)}) copy-start(s32[1024]{0:T(1024)} %pad_clamp_fusion) | copy-start | bytes 12292
  137.4 11.7 %all-to-all-start.3 = ((bf16[8,25,768]{2,1,0:T(8,128)(2,1)}), bf16[8,25,768]{2,1,0:T(8,128)(2,1)S(1)}, u32[]{:S(2)}, u32[]{:S(2)}) async-start(bf16[8,25,768]{2,1,0:T(8,128)(2,1)} %reshape.329), calls=%async_computation.3 | async-start | bytes 786432 | tf_op jit(solution)/shard_map/all_to_all | solution.py:233
  140.9 234.5 %reduce-scatter.2.cloned.1.call-start = ((), (), s32[]{:S(2)}) async-start(), calls=%async_computation.7 | async-start | bytes 5308416 | tf_op jit(solution)/shard_map/reduce_scatter | solution.py:293
  157.6 2.8 copy-start.1
  157.6 4.4 copy-start.36
  160.4 3.1 copy-start.16
  162.0 2.6 copy-start.5
  165.1 4.1 copy-start.7
  176.0 6.3 %copy-start.14 = (bf16[12,64,197]{2,1,0:T(8,128)(2,1)S(1)}, bf16[12,64,197]{2,1,0:T(8,128)(2,1)}, u32[]{:S(2)}) copy-start(bf16[12,64,197]{2,1,0:T(8,128)(2,1)} %copy-done.13) | copy-start | bytes 907780
  180.9 1.9 copy-start.38
  187.0 195.0 %all-gather.25.cloned.1.call-start = ((), (), s32[]{:S(2)}) async-start(), calls=%async_computation.14 | async-start | bytes 1622016 | tf_op jit(solution)/shard_map/all_gather | solution.py:308
  193.2 220.4 %all-reduce.3.cloned.1.call-start = ((), (), s32[]{:S(2)}) async-start(), calls=%async_computation.8 | async-start | bytes 1179648 | tf_op jit(solution)/shard_map/psum | solution.py:307
  194.3 6.5 %copy-start.57 = (bf16[1,768,1536]{2,1,0:T(8,128)(2,1)S(1)}, bf16[1,768,1536]{2,1,0:T(8,128)(2,1)}, u32[]{:S(2)}) copy-start(bf16[1,768,1536]{2,1,0:T(8,128)(2,1)} %param.29) | copy-start | bytes 7077892
  272.3 1.5 copy-start.9
  329.7 5.6 %copy-start.59 = (bf16[768,1536]{1,0:T(8,128)(2,1)S(1)}, bf16[768,1536]{1,0:T(8,128)(2,1)}, u32[]{:S(2)}) copy-start(bf16[768,1536]{1,0:T(8,128)(2,1)} %add_convert_fusion.11) | copy-start | bytes 7077892
  341.8 5.6 %copy-start.60 = (bf16[768,1536]{1,0:T(8,128)(2,1)S(1)}, bf16[768,1536]{1,0:T(8,128)(2,1)}, u32[]{:S(2)}) copy-start(bf16[768,1536]{1,0:T(8,128)(2,1)} %add_convert_fusion.10) | copy-start | bytes 7077892
  353.9 5.6 %copy-start.58 = (bf16[768,1536]{1,0:T(8,128)(2,1)S(1)}, bf16[768,1536]{1,0:T(8,128)(2,1)}, u32[]{:S(2)}) copy-start(bf16[768,1536]{1,0:T(8,128)(2,1)} %add_convert_fusion.4) | copy-start | bytes 7077892
  369.4 3.1 copy-start.3
  375.4 3.7 copy-start.4
  375.4 64.3 %all-gather.21.cloned.1.call-start = ((), (), s32[]{:S(2)}) async-start(), calls=%async_computation.12 | async-start | bytes 1327104 | tf_op jit(solution)/shard_map/all_gather | solution.py:319
  379.1 34.5 %copy-start.24 = (f32[96,768]{1,0:T(8,128)S(1)}, f32[96,768]{1,0:T(8,128)}, u32[]{:S(2)}) copy-start(f32[96,768]{1,0:T(8,128)} %param.33) | copy-start | bytes 884740
  382.0 33.6 %copy-start.33 = (f32[768,8]{0,1:T(8,128)S(1)}, f32[768,8]{0,1:T(8,128)}, u32[]{:S(2)}) copy-start(f32[768,8]{0,1:T(8,128)} %param.31) | copy-start | bytes 73732
  382.0 36.4 %copy-start.21 = (f32[96,2304]{1,0:T(8,128)S(1)}, f32[96,2304]{1,0:T(8,128)}, u32[]{:S(2)}) copy-start(f32[96,2304]{1,0:T(8,128)} %param.32) | copy-start | bytes 2654212
  413.6 4.8 copy-start.10
  415.5 60.3 %all-gather.19.cloned.1.call-start = ((), (), s32[]{:S(2)}) async-start(), calls=%async_computation.11 | async-start | bytes 3981312 | tf_op jit(solution)/shard_map/all_gather | solution.py:318
  417.9 3.0 copy-start.26
  418.4 3.5 copy-start.30
  418.4 3.5 copy-start.32
  418.4 3.5 copy-start.44
  442.9 2.9 copy-start.18
  475.8 5.7 %copy-start.8 = (bf16[768,2304]{1,0:T(8,128)(2,1)S(1)}, bf16[768,2304]{1,0:T(8,128)(2,1)}, u32[]{:S(2)}) copy-start(bf16[768,2304]{1,0:T(8,128)(2,1)} %all-gather.19.cloned.1.call-done) | copy-start | bytes 10616836
  493.3 7.2 %copy-start.61 = (bf16[768,2304]{1,0:T(8,128)(2,1)S(1)}, bf16[768,2304]{1,0:T(8,128)(2,1)}, u32[]{:S(2)}) copy-start(bf16[768,2304]{1,0:T(8,128)(2,1)} %add_convert_fusion.3) | copy-start | bytes 10616836
  508.3 7.3 %copy-start.62 = (bf16[768,2304]{1,0:T(8,128)(2,1)S(1)}, bf16[768,2304]{1,0:T(8,128)(2,1)}, u32[]{:S(2)}) copy-start(bf16[768,2304]{1,0:T(8,128)(2,1)} %add_convert_fusion.2) | copy-start | bytes 10616836
  (12 other events, 12.3 us)
Sparse Core Ops, SparseCore 0:
  9.9 36.5 all-gather.10
  48.4 23.9 all-gather.12
  88.4 30.1 all-gather.14
  125.6 30.1 all-gather.16
  157.8 88.5 all-gather.22
  249.7 52.1 reduce-scatter.1
  305.4 54.8 all-gather.24
  375.5 38.0 all-reduce.2
  416.1 23.5 all-gather.20
  442.0 33.8 all-gather.18

commit v2 on v1

--- a/solution.py
+++ b/solution.py
@@ -155,6 +155,7 @@
     moment_pair = jnp.concatenate(
         [w_in_momentum[0].astype(jnp.bfloat16), w_out_momentum[0].astype(jnp.bfloat16)], axis=1
     )
+    every_moment = lax.all_gather(moment_pair, "dp", axis=0, tiled=True)
     token_float = tokens.astype(jnp.float32)
     scaled_one, inverse_one, normed_one = layer_stats(token_float, ln_gains[0], ln_biases[0])
     attn_in = normed_one.astype(jnp.bfloat16)
@@ -253,6 +254,7 @@
     )
     router_local = lax.dot_general(normed, logit_grad, contract_first, precision=highest)
     middle_grad = input_grad(cot_float, normed_grad, scaled, inverse, ln_gains[1])
+    middle_grad, every_moment = lax.optimization_barrier((middle_grad, every_moment))
     middle_rounded = middle_grad.astype(jnp.bfloat16)
     mixed_grad = lax.dot_general(
         middle_rounded, full_out, contract_last, preferred_element_type=jnp.float32
@@ -280,6 +282,7 @@
         .astype(jnp.bfloat16)
         .reshape(token_count, 3 * model_width)
     )
+    qkv_grad, every_row, every_grad = lax.optimization_barrier((qkv_grad, every_row, every_grad))
     attn_in_grad = lax.dot_general(
         qkv_grad, full_qkv, contract_last, preferred_element_type=jnp.float32
     )
@@ -318,31 +321,55 @@
     whole_qkv = lax.all_gather(moment_qkv.astype(jnp.bfloat16), "expert", axis=0, tiled=True)
     whole_out = lax.all_gather(moment_out.astype(jnp.bfloat16), "expert", axis=0, tiled=True)
     row_base = lax.axis_index("dp") * dp_share
-    every_moment = lax.all_gather(moment_pair, "dp", axis=0, tiled=True)
     every_preact = jnp.dot(every_row, first_weight, preferred_element_type=jnp.float32)
     every_active = jax.nn.gelu(every_preact, approximate=False).astype(jnp.bfloat16)
     every_act_grad = jnp.dot(every_grad, second_weight, preferred_element_type=jnp.float32)
     every_pre_grad = (every_act_grad * gelu_slope(every_preact)).astype(jnp.bfloat16)
-    whole_first = lax.dot_general(
-        every_row, every_pre_grad, contract_first, preferred_element_type=jnp.float32
-    )
-    whole_second = lax.dot_general(
-        every_grad, every_active, contract_first, preferred_element_type=jnp.float32
-    )
-    grad_first = lax.dynamic_slice_in_dim(whole_first, row_base, dp_share, 0)
-    grad_second = lax.dynamic_slice_in_dim(whole_second, row_base, dp_share, 0)
+    dp_count = lax.axis_size("dp")
+    dp_half = dp_count // 2
+    role = lax.axis_index("dp") // dp_half
+    pair_index = lax.axis_index("dp") % dp_half
+    does_first = role == 0
+    role_left = jnp.where(does_first, every_row, every_grad)
+    role_right = jnp.where(does_first, every_pre_grad, every_active)
+    role_moment = jnp.where(
+        does_first, every_moment[:, :hidden_units], every_moment[:, hidden_units:]
+    )
+    role_grad = lax.dot_general(
+        role_left, role_right, contract_first, preferred_element_type=jnp.float32
+    )
+    role_iter = ortho_rows(
+        decay_rate * role_moment.astype(jnp.float32) + role_grad,
+        pair_index * (2 * dp_share),
+        2 * dp_share,
+    )
+    near_rows = lax.ppermute(
+        lax.dynamic_slice_in_dim(role_iter, role * dp_share, dp_share, 0),
+        "dp",
+        [(r * dp_half + k, 2 * k + r) for r in range(2) for k in range(dp_half)],
+    )
+    far_rows = lax.ppermute(
+        lax.dynamic_slice_in_dim(role_iter, (1 - role) * dp_share, dp_share, 0),
+        "dp",
+        [(r * dp_half + k, 2 * k + 1 - r) for r in range(2) for k in range(dp_half)],
+    )
+    is_even = lax.axis_index("dp") % 2 == 0
+    iter_first = jnp.where(is_even, near_rows, far_rows)
+    iter_second = jnp.where(is_even, far_rows, near_rows)
+    grad_first = lax.dot_general(
+        lax.dynamic_slice_in_dim(every_row, row_base, dp_share, 1),
+        every_pre_grad,
+        contract_first,
+        preferred_element_type=jnp.float32,
+    )
+    grad_second = lax.dot_general(
+        lax.dynamic_slice_in_dim(every_grad, row_base, dp_share, 1),
+        every_active,
+        contract_first,
+        preferred_element_type=jnp.float32,
+    )
     moment_first = decay_rate * w_in_momentum[0] + grad_first
     moment_second = decay_rate * w_out_momentum[0] + grad_second
-    iter_first = ortho_rows(
-        decay_rate * every_moment[:, :hidden_units].astype(jnp.float32) + whole_first,
-        row_base,
-        dp_share,
-    )
-    iter_second = ortho_rows(
-        decay_rate * every_moment[:, hidden_units:].astype(jnp.float32) + whole_second,
-        row_base,
-        dp_share,
-    )
     expert_share = qkv_weight.shape[0]
     expert_base = lax.axis_index("expert") * expert_share
     iter_out = ortho_rows(whole_out.astype(jnp.float32), expert_base, expert_share)

time: 562 us -> 570 us (1.014)
  waiting for transfers between devices: 158 us -> 204 us
  matrix products: 268 us -> 235 us
  blocking collectives: 10.7 us -> 0 us
  starting transfers between devices: 11.3 us -> 22 us
  other arithmetic: 53.7 us -> 46.5 us
    all_gather x1, waiting for transfers between devices: 0.01 us -> 32.3 us  [body(): every_grad = lax.all_gather(grad_rows, 'dp', axis=0, tiled=True)]
    all_gather x1, waiting for transfers between devices: 35.3 us -> 3.74 us  [body(): every_moment = lax.all_gather(moment_pair, 'dp', axis=0, tiled=True)]
    all_gather x1, waiting for transfers between devices: 0.01 us -> 31.5 us  [body(): lax.all_gather(jnp.concatenate([router_local.T, norm_local], axis=0), ('d...]
    dot_general x20 -> x15, matrix products: 105 us -> 89.8 us  [ortho_rows(): jnp.dot(mixer, iterate, preferred_element_type=jnp.float32)]
    all_gather x1, waiting for transfers between devices: 0.01 us -> 13.4 us  [body(): every_row = lax.all_gather(arrived_rows, 'dp', axis=0, tiled=True)]
    dot_general x20 -> x15, matrix products: 79.2 us -> 66.2 us  [ortho_rows(): lax.dot_general(iterate, iterate, contract_last, preferred_element_type=j...]
    all_gather x1, waiting for transfers between devices: 15.6 us -> 2.91 us  [body(): lax.all_gather(moment_qkv.astype(jnp.bfloat16), 'expert', axis=0, tiled=T...]
    dot_general x2 -> x4, matrix products: 28.5 us -> 17.7 us  [the longest x1 8.4 us: body(): lax.dot_general(role_left, role_right, contract_first, preferred_element_...]
  transfers between devices with their start and end apart: 13 -> 16, of which waited for: 9 -> 14; matrix products, arithmetic and copies ran while one was open for 50% -> 41% of each run, Pallas kernels for 0% -> 0%
where the time goes in v2:
time: 570 us; the launch traced here: 561 us
  matrix products  235 us (41%)
  waiting for transfers between devices  204 us (36%)
  other arithmetic  46.5 us (8%)
  local copies, waits for them, and re-layouts  33.9 us (6%)
  starting transfers between devices  22 us (4%)
  between operations  18.4 us (3%)
    dot_general x15, matrix products, ortho_rows(): jnp.dot(mixer, iterate, preferred_element_type=jnp.float32)  89.8 us
    dot_general x15, matrix products, ortho_rows(): lax.dot_general(iterate, iterate, contract_last, preferred_element_type=j...  66.2 us
    psum x1, waiting for transfers between devices, body(): attention_total = lax.psum(attention_share, 'dp').astype(jnp.float32)  39.5 us
    all_gather x1, waiting for transfers between devices, body(): every_grad = lax.all_gather(grad_rows, 'dp', axis=0, tiled=True)  32.3 us
    all_gather x1, waiting for transfers between devices, body(): lax.all_gather(jnp.concatenate([router_local.T, norm_local], axis=0), ('d...  31.5 us
    all_gather x1, waiting for transfers between devices, body(): lax.all_gather(qkv_weight, 'expert', axis=0, tiled=True)  28.9 us
    all_gather x1, waiting for transfers between devices, body(): lax.all_gather(out_weight, 'expert', axis=0, tiled=True)  16.8 us
    all_gather x1, waiting for transfers between devices, body(): lax.all_gather(moment_out.astype(jnp.bfloat16), 'expert', axis=0, tiled=T...  16.8 us
  transfers between devices with their start and end apart: 16, of which 14 were waited for; matrix products, arithmetic and copies ran while one was open for 41% of the time, Pallas kernels for 0%

profile of v2, /device:TPU:0, one launch (start us, length us, event | category | flops | bytes accessed | tf_op | source)
XLA Modules:
  0.0 560.6 jit_solution(17251825815001008520)
XLA Ops:
  17.6 28.9 %all-gather.11.cloned.1.call-done = bf16[768,2304]{1,0:T(8,128)(2,1)} async-done(((bf16[96,2304]{1,0:T(8,128)(2,1)}), bf16[768,2304]{1,0:T(8,128)(2,1)}) %all-gather.11.cloned.1.call-update) | async-done | bytes 3538960 | tf_op jit(solution)/shard_map/all_gather | solution.py:152
  46.5 3.0 convolution_convert_fusion.1
  52.1 3.4 convolution_convert_fusion.19
  55.5 16.8 %all-gather.13.cloned.1.call-done = bf16[768,768]{1,0:T(8,128)(2,1)} async-done(((bf16[96,768]{1,0:T(8,128)(2,1)}), bf16[768,768]{1,0:T(8,128)(2,1)}) %all-gather.13.cloned.1.call-update) | async-done | bytes 1179664 | tf_op jit(solution)/shard_map/all_gather | solution.py:153
  75.7 3.5 all-to-all-start
  84.1 3.3 all-to-all-done
  91.1 3.2 fusion.77
  95.2 3.5 all-to-all-start.1
  99.6 4.6 gather_fusion.1
  104.4 2.5 all-to-all-done.1
  111.5 3.5 all-to-all-start.2
  115.0 4.4 fusion.29
  120.0 3.2 all-to-all-done.2
  123.4 4.9 fusion.74
  130.1 3.5 all-to-all-start.3
  135.1 6.7 %all-to-all-done.3 = bf16[8,25,768]{2,1,0:T(8,128)(2,1)S(1)} async-done(((bf16[8,25,768]{2,1,0:T(8,128)(2,1)}), bf16[8,25,768]{2,1,0:T(8,128)(2,1)S(1)}, u32[]{:S(2)}, u32[]{:S(2)}) %all-to-all-start.3) | async-done | bytes 307232 | tf_op jit(solution)/shard_map/all_to_all | solution.py:234
  145.4 3.1 reshape.336
  148.5 2.7 reduce_sum.216
  154.6 2.9 multiply_reduce_fusion.2
  160.1 3.7 all-gather.15.cloned.1.call-done
  164.6 3.5 fusion.80
  170.1 4.3 fusion.81
  174.4 4.8 fusion.82
  182.0 13.4 %all-gather.17.cloned.1.call-done = bf16[800,768]{1,0:T(8,128)(2,1)} async-done(((bf16[200,768]{1,0:T(8,128)(2,1)}), bf16[800,768]{1,0:T(8,128)(2,1)}) %all-gather.17.cloned.1.call-update) | async-done | bytes 1228816 | tf_op jit(solution)/shard_map/all_gather | solution.py:188
  195.4 32.3 %all-gather.19.cloned.1.call-done = bf16[800,768]{1,0:T(8,128)(2,1)} async-done(((bf16[200,768]{1,0:T(8,128)(2,1)}), bf16[800,768]{1,0:T(8,128)(2,1)}) %all-gather.19.cloned.1.call-update) | async-done | bytes 1228816 | tf_op jit(solution)/shard_map/all_gather | solution.py:228
  227.7 2.6 convolution_convert_fusion
  230.3 2.8 pad_maximum_fusion
  234.4 13.9 %fusion.12 = (bf16[800,1536]{1,0:T(8,128)(2,1)S(1)}, f32[800,1536]{1,0:T(8,128)S(1)}) fusion(bf16[800,768]{1,0:T(8,128)(2,1)S(1)} %copy-done.32, bf16[1,768,1536]{2,1,0:T(8,128)(2,1)} %param.28), kind=kOutput, calls=%fused_computation.26 | convolution fusion | flops 1967308800 | bytes 10960896 | tf_op jit(solution)/shard_map/dot_general | solution.py:324
  248.4 4.2 fusion.9
  252.6 8.4 %multiply_reduce_fusion = (f32[]{:T(128)}, f32[768,1536]{1,0:T(8,128)}) fusion(bf16[800,1536]{1,0:T(8,128)(2,1)S(1)} %fusion.9, bf16[800,1536]{1,0:T(8,128)(2,1)S(1)} %get-tuple-element.78, pred[]{:T(512)S(6)} %eq.112, bf16[800,768]{1,0:T(8,128)(2,1)S(1)} %copy-done.32, bf16[800,768]{1,0:T(8,128)(2,1)S(1)} %copy-done.33, ...), kind=kOutput, calls=%fused_computation.48 | convolution fusion | flops 1896357888 | bytes 16811524 | tf_op jit(solution)/shard_map/dot_general | solution.py:338
  264.5 5.9 %convolution_convert_fusion.17 = bf16[768,768]{1,0:T(8,128)(2,1)S(1)} fusion(f32[768,1536]{1,0:T(8,128)} %get-tuple-element.81, f32[]{:T(128)S(6)} %add.379), kind=kOutput, calls=%fused_computation.122 | convolution fusion | flops 1814888448 | bytes 5898244 | tf_op jit(solution)/shard_map/dot_general | solution.py:90
  270.4 8.2 %add_convert_fusion.7 = bf16[768,1536]{1,0:T(8,128)(2,1)} fusion(bf16[768,768]{1,0:T(8,128)(2,1)S(1)} %convolution_convert_fusion.17, f32[768,1536]{1,0:T(8,128)} %get-tuple-element.81, f32[]{:T(128)S(6)} %add.379), kind=kOutput, calls=%fused_computation.46 | convolution fusion | flops 2730295296 | bytes 8257540 | tf_op jit(solution)/shard_map/dot_general | solution.py:103
  278.6 4.4 convolution_convert_fusion.16
  283.0 6.6 %add_convert_fusion.6 = bf16[768,1536]{1,0:T(8,128)(2,1)} fusion(bf16[768,1536]{1,0:T(8,128)(2,1)} %add_convert_fusion.7, bf16[768,768]{1,0:T(8,128)(2,1)S(1)} %convolution_convert_fusion.16), kind=kOutput, calls=%fused_computation.45 | convolution fusion | flops 2725576704 | bytes 5898240 | tf_op jit(solution)/shard_map/dot_general | solution.py:103
  289.7 4.4 convolution_convert_fusion.15
  294.1 6.5 %add_convert_fusion.5 = bf16[768,1536]{1,0:T(8,128)(2,1)} fusion(bf16[768,1536]{1,0:T(8,128)(2,1)} %add_convert_fusion.6, bf16[768,768]{1,0:T(8,128)(2,1)S(1)} %convolution_convert_fusion.15), kind=kOutput, calls=%fused_computation.44 | convolution fusion | flops 2725576704 | bytes 5898240 | tf_op jit(solution)/shard_map/dot_general | solution.py:103
  300.6 4.4 convolution_convert_fusion.14
  305.0 6.5 %add_convert_fusion.4 = bf16[768,1536]{1,0:T(8,128)(2,1)} fusion(bf16[768,1536]{1,0:T(8,128)(2,1)} %add_convert_fusion.5, bf16[768,768]{1,0:T(8,128)(2,1)S(1)} %convolution_convert_fusion.14), kind=kOutput, calls=%fused_computation.43 | convolution fusion | flops 2725576704 | bytes 5898240 | tf_op jit(solution)/shard_map/dot_general | solution.py:103
  311.5 5.4 convolution_convert_fusion.13
  317.0 4.3 fusion.24
  323.5 6.0 %collective-permute-start = (bf16[192,1536]{1,0:T(8,128)(2,1)}, bf16[192,1536]{1,0:T(8,128)(2,1)}, u32[]{:S(2)}, u32[]{:S(2)}) collective-permute-start(bf16[192,1536]{1,0:T(8,128)(2,1)} %get-tuple-element.65), channel_id=1, source_target_pairs={{0,0},{8,16},{16,8},{24,24},{1,1},{9,17},{17,9},{25,25},{2,2},{10,... | collective-permute-start | bytes 1769480 | tf_op jit(solution)/shard_map/ppermute | solution.py:346
  329.5 2.8 fusion.172
  340.7 3.3 fusion.83
  344.0 31.5 %all-gather.25.cloned.1.call-done = f32[32,12,768]{2,1,0:T(8,128)} async-done(((f32[1,12,768]{2,1,0:T(8,128)}), f32[32,12,768]{2,1,0:T(8,128)}) %all-gather.25.cloned.1.call-update) | async-done | bytes 1179664 | tf_op jit(solution)/shard_map/all_gather | solution.py:311
  377.0 39.5 %all-reduce.3.cloned.1.call-done = bf16[96,3072]{1,0:T(8,128)(2,1)} async-done(((bf16[96,3072]{1,0:T(8,128)(2,1)}), bf16[96,3072]{1,0:T(8,128)(2,1)}) %all-reduce.3.cloned.1.call-update) | async-done | bytes 589840 | tf_op jit(solution)/shard_map/psum | solution.py:310
  425.8 16.8 %all-gather.23.cloned.1.call-done = bf16[768,768]{1,0:T(8,128)(2,1)} async-done(((bf16[96,768]{1,0:T(8,128)(2,1)}), bf16[768,768]{1,0:T(8,128)(2,1)}) %all-gather.23.cloned.1.call-update) | async-done | bytes 1179664 | tf_op jit(solution)/shard_map/all_gather | solution.py:322
  442.6 2.5 fusion.33
  445.8 3.9 convolution_convert_fusion.11
  449.7 4.5 add_convert_fusion.18
  456.3 4.2 add_convert_fusion.16
  462.7 4.2 add_convert_fusion.14
  469.1 4.2 add_convert_fusion.12
  475.8 2.9 all-gather.21.cloned.1.call-done
  478.8 4.6 fusion.2
  484.0 6.0 %convolution_convert_fusion.6 = bf16[768,768]{1,0:T(8,128)(2,1)S(1)} fusion(bf16[768,2304]{1,0:T(8,128)(2,1)} %all-gather.21.cloned.1.call-done, f32[]{:T(128)S(6)} %add.353), kind=kOutput, calls=%fused_computation.111 | convolution fusion | flops 2723807232 | bytes 4718596 | tf_op jit(solution)/shard_map/dot_general | solution.py:90
  490.1 9.0 %add_convert_fusion.3 = bf16[768,2304]{1,0:T(8,128)(2,1)} fusion(bf16[768,768]{1,0:T(8,128)(2,1)S(1)} %convolution_convert_fusion.6, f32[]{:T(128)S(6)} %add.353, bf16[768,2304]{1,0:T(8,128)(2,1)} %all-gather.21.cloned.1.call-done), kind=kOutput, calls=%fused_computation.16 | convolution fusion | flops 3644522496 | bytes 8257540 | tf_op jit(solution)/shard_map/dot_general | solution.py:103
  499.1 6.1 %convolution_convert_fusion.5 = bf16[768,768]{1,0:T(8,128)(2,1)S(1)} fusion(bf16[768,2304]{1,0:T(8,128)(2,1)} %add_convert_fusion.3), kind=kOutput, calls=%fused_computation.110 | convolution fusion | flops 2718498816 | bytes 4718592 | tf_op jit(solution)/shard_map/dot_general | solution.py:90
  505.2 8.7 %add_convert_fusion.2 = bf16[768,2304]{1,0:T(8,128)(2,1)} fusion(bf16[768,2304]{1,0:T(8,128)(2,1)} %add_convert_fusion.3, bf16[768,768]{1,0:T(8,128)(2,1)S(1)} %convolution_convert_fusion.5), kind=kOutput, calls=%fused_computation.15 | convolution fusion | flops 3633905664 | bytes 8257536 | tf_op jit(solution)/shard_map/dot_general | solution.py:103
  513.8 6.0 %convolution_convert_fusion.4 = bf16[768,768]{1,0:T(8,128)(2,1)S(1)} fusion(bf16[768,2304]{1,0:T(8,128)(2,1)} %add_convert_fusion.2), kind=kOutput, calls=%fused_computation.109 | convolution fusion | flops 2718498816 | bytes 4718592 | tf_op jit(solution)/shard_map/dot_general | solution.py:90
  519.9 8.6 %add_convert_fusion.1 = bf16[768,2304]{1,0:T(8,128)(2,1)} fusion(bf16[768,2304]{1,0:T(8,128)(2,1)} %add_convert_fusion.2, bf16[768,768]{1,0:T(8,128)(2,1)S(1)} %convolution_convert_fusion.4), kind=kOutput, calls=%fused_computation.14 | convolution fusion | flops 3633905664 | bytes 8257536 | tf_op jit(solution)/shard_map/dot_general | solution.py:103
  528.4 6.1 %convolution_convert_fusion.3 = bf16[768,768]{1,0:T(8,128)(2,1)S(1)} fusion(bf16[768,2304]{1,0:T(8,128)(2,1)} %add_convert_fusion.1), kind=kOutput, calls=%fused_computation.108 | convolution fusion | flops 2718498816 | bytes 4718592 | tf_op jit(solution)/shard_map/dot_general | solution.py:90
  534.5 8.9 %add_convert_fusion = bf16[768,2304]{1,0:T(8,128)(2,1)} fusion(bf16[768,2304]{1,0:T(8,128)(2,1)} %add_convert_fusion.1, bf16[768,768]{1,0:T(8,128)(2,1)S(1)} %convolution_convert_fusion.3), kind=kOutput, calls=%fused_computation.13 | convolution fusion | flops 3633905664 | bytes 8257536 | tf_op jit(solution)/shard_map/dot_general | solution.py:103
  543.4 6.1 %convolution_convert_fusion.2 = bf16[768,768]{1,0:T(8,128)(2,1)S(1)} fusion(bf16[768,2304]{1,0:T(8,128)(2,1)} %add_convert_fusion), kind=kOutput, calls=%fused_computation.107 | convolution fusion | flops 2718498816 | bytes 4718592 | tf_op jit(solution)/shard_map/dot_general | solution.py:90
  549.5 4.0 fusion.23
  (270 shorter events, 84.0 us)
Async XLA Ops:
  7.2 39.3 %all-gather.11.cloned.1.call-start = ((), (), s32[]{:S(2)}) async-start(), calls=%async_computation.5 | async-start | bytes 3981312 | tf_op jit(solution)/shard_map/all_gather | solution.py:152
  7.9 64.4 %all-gather.13.cloned.1.call-start = ((), (), s32[]{:S(2)}) async-start(), calls=%async_computation.6 | async-start | bytes 1327104 | tf_op jit(solution)/shard_map/all_gather | solution.py:153
  8.7 155.2 %all-gather.15.cloned.1.call-start = ((), (), s32[]{:S(2)}) async-start(), calls=%async_computation.7 | async-start | bytes 5898240 | tf_op jit(solution)/shard_map/all_gather | solution.py:158
  11.6 4.7 copy-start.38
  11.6 4.7 copy-start.36
  11.7 5.0 copy-start
  16.4 58.0 %copy-start.49 = (f32[768]{0:T(1024)}, f32[768]{0:T(1024)S(1)}, u32[]{:S(2)}) copy-start(f32[768]{0:T(1024)S(1)} %get-tuple-element.47) | copy-start | bytes 9220
  16.6 57.8 %copy-start.59 = (s32[197]{0:T(256)}, s32[197]{0:T(256)S(1)}, u32[]{:S(2)}) copy-start(s32[197]{0:T(256)S(1)} %get-tuple-element.41) | copy-start | bytes 2368
  16.6 57.8 %copy-start.61 = (s32[197]{0:T(256)}, s32[197]{0:T(256)S(1)}, u32[]{:S(2)}) copy-start(s32[197]{0:T(256)S(1)} %get-tuple-element.42) | copy-start | bytes 2368
  17.0 32.4 %copy-start.47 = (f32[197]{0:T(256)}, f32[197]{0:T(256)S(1)}, u32[]{:S(2)}) copy-start(f32[197]{0:T(256)S(1)} %add_rsqrt_fusion.1) | copy-start | bytes 2368
  50.1 5.4 copy-start.6
  55.5 20.2 %copy-start.17 = (bf16[12,64,197]{2,1,0:T(8,128)(2,1)}, bf16[12,64,197]{2,1,0:T(8,128)(2,1)S(1)}, u32[]{:S(2)}) copy-start(bf16[12,64,197]{2,1,0:T(8,128)(2,1)S(1)} %convolution_convert_fusion.19) | copy-start | bytes 907780
  72.3 7.6 %copy-start.19 = (bf16[197,768]{1,0:T(8,128)(2,1)S(1)}, bf16[197,768]{1,0:T(8,128)(2,1)}, u32[]{:S(2)}) copy-start(bf16[197,768]{1,0:T(8,128)(2,1)} %param.20) | copy-start | bytes 907780
  74.4 9.1 %copy-start.44 = (f32[197]{0:T(256)}, f32[197]{0:T(256)S(1)}, u32[]{:S(2)}) copy-start(f32[197]{0:T(256)S(1)} %add_rsqrt_fusion) | copy-start | bytes 2368
  75.7 11.7 %all-to-all-start = ((bf16[8,25,768]{2,1,0:T(8,128)(2,1)}), bf16[8,25,768]{2,1,0:T(8,128)(2,1)S(1)}, u32[]{:S(2)}, u32[]{:S(2)}) async-start(bf16[8,25,768]{2,1,0:T(8,128)(2,1)} %reshape.322), calls=%async_computation | async-start | bytes 786432 | tf_op jit(solution)/shard_map/all_to_all | solution.py:186
  87.5 6.8 %copy-start.9 = (bf16[200,768]{1,0:T(8,128)(2,1)}, bf16[200,768]{1,0:T(8,128)(2,1)S(1)}, u32[]{:S(2)}) copy-start(bf16[200,768]{1,0:T(8,128)(2,1)S(1)} %reshape.323) | copy-start | bytes 921604
  87.5 3.5 copy-start.30
  91.1 7.8 %copy-start.29 = (f32[768,8]{0,1:T(8,128)S(1)}, f32[768,8]{0,1:T(8,128)}, u32[]{:S(2)}) copy-start(f32[768,8]{0,1:T(8,128)} %param.27) | copy-start | bytes 73732
  91.1 7.8 %copy-start.45 = (f32[197]{0:T(256)S(1)}, f32[197]{0:T(256)}, u32[]{:S(2)}) copy-start(f32[197]{0:T(256)} %copy-done.44) | copy-start | bytes 2368
  91.1 7.8 %copy-start.50 = (f32[768]{0:T(1024)S(1)}, f32[768]{0:T(1024)}, u32[]{:S(2)}) copy-start(f32[768]{0:T(1024)} %copy-done.49) | copy-start | bytes 9220
  95.2 11.7 %all-to-all-start.1 = ((bf16[8,25,768]{2,1,0:T(8,128)(2,1)}), bf16[8,25,768]{2,1,0:T(8,128)(2,1)S(1)}, u32[]{:S(2)}, u32[]{:S(2)}) async-start(bf16[8,25,768]{2,1,0:T(8,128)(2,1)} %reshape.324), calls=%async_computation.1 | async-start | bytes 786432 | tf_op jit(solution)/shard_map/all_to_all | solution.py:194
  98.6 96.8 %all-gather.17.cloned.1.call-start = ((), (), s32[]{:S(2)}) async-start(), calls=%async_computation.8 | async-start | bytes 1536000 | tf_op jit(solution)/shard_map/all_gather | solution.py:188
  99.6 7.4 %copy-start.42 = (s32[1024]{0:T(1024)S(1)}, s32[1024]{0:T(1024)}, u32[]{:S(2)}) copy-start(s32[1024]{0:T(1024)} %pad_clamp_fusion) | copy-start | bytes 12292
  110.0 9.4 %copy-start.23 = (f32[197,1]{1,0:T(8,128)}, f32[197,1]{1,0:T(8,128)S(1)}, u32[]{:S(2)}) copy-start(f32[197,1]{1,0:T(8,128)S(1)} %get-tuple-element.61) | copy-start | bytes 2368
  111.5 11.7 %all-to-all-start.2 = ((bf16[8,25,768]{2,1,0:T(8,128)(2,1)}), bf16[8,25,768]{2,1,0:T(8,128)(2,1)S(1)}, u32[]{:S(2)}, u32[]{:S(2)}) async-start(bf16[8,25,768]{2,1,0:T(8,128)(2,1)} %reshape.327), calls=%async_computation.2 | async-start | bytes 786432 | tf_op jit(solution)/shard_map/all_to_all | solution.py:226
  114.9 8.4 %copy-start.15 = (f32[200,1536]{1,0:T(8,128)S(1)}, f32[200,1536]{1,0:T(8,128)}, u32[]{:S(2)}) copy-start(f32[200,1536]{1,0:T(8,128)} %copy-done.14) | copy-start | bytes 3686404
  123.3 5.0 copy-start.21
  123.3 10.3 %copy-start.24 = (f32[197,1]{1,0:T(8,128)S(1)}, f32[197,1]{1,0:T(8,128)}, u32[]{:S(2)}) copy-start(f32[197,1]{1,0:T(8,128)} %copy-done.23) | copy-start | bytes 2368
  123.3 10.3 %copy-start.27 = (f32[197,1]{1,0:T(8,128)S(1)}, f32[197,1]{1,0:T(8,128)}, u32[]{:S(2)}) copy-start(f32[197,1]{1,0:T(8,128)} %broadcast_subtract_fusion) | copy-start | bytes 2368
  123.3 10.4 %copy-start.46 = (f32[197]{0:T(256)S(1)}, f32[197]{0:T(256)}, u32[]{:S(2)}) copy-start(f32[197]{0:T(256)} %copy-done.44) | copy-start | bytes 2368
  123.4 10.4 %copy-start.51 = (f32[768]{0:T(1024)S(1)}, f32[768]{0:T(1024)}, u32[]{:S(2)}) copy-start(f32[768]{0:T(1024)} %copy-done.49) | copy-start | bytes 9220
  123.4 10.4 %copy-start.55 = (s32[197,1]{0,1:T(1,128)S(1)}, s32[197,1]{0,1:T(1,128)}, u32[]{:S(2)}) copy-start(s32[197,1]{0,1:T(1,128)} %get-tuple-element.68) | copy-start | bytes 2368
  123.4 10.4 %copy-start.56 = (s32[197,1]{0,1:T(1,128)S(1)}, s32[197,1]{0,1:T(1,128)}, u32[]{:S(2)}) copy-start(s32[197,1]{0,1:T(1,128)} %get-tuple-element.69) | copy-start | bytes 2368
  128.3 13.7 %copy-start.43 = (s32[1024]{0:T(1024)S(1)}, s32[1024]{0:T(1024)}, u32[]{:S(2)}) copy-start(s32[1024]{0:T(1024)} %pad_clamp_fusion) | copy-start | bytes 12292
  130.1 11.7 %all-to-all-start.3 = ((bf16[8,25,768]{2,1,0:T(8,128)(2,1)}), bf16[8,25,768]{2,1,0:T(8,128)(2,1)S(1)}, u32[]{:S(2)}, u32[]{:S(2)}) async-start(bf16[8,25,768]{2,1,0:T(8,128)(2,1)} %reshape.329), calls=%async_computation.3 | async-start | bytes 786432 | tf_op jit(solution)/shard_map/all_to_all | solution.py:234
  133.6 94.2 %all-gather.19.cloned.1.call-start = ((), (), s32[]{:S(2)}) async-start(), calls=%async_computation.9 | async-start | bytes 1536000 | tf_op jit(solution)/shard_map/all_gather | solution.py:228
  135.1 203.0 %reduce-scatter.2.cloned.1.call-start = ((), (), s32[]{:S(2)}) async-start(), calls=%async_computation.10 | async-start | bytes 5308416 | tf_op jit(solution)/shard_map/reduce_scatter | solution.py:296
  154.6 9.3 %copy-start.5 = (bf16[768,768]{1,0:T(8,128)(2,1)S(1)}, bf16[768,768]{1,0:T(8,128)(2,1)}, u32[]{:S(2)}) copy-start(bf16[768,768]{1,0:T(8,128)(2,1)} %all-gather.13.cloned.1.call-done) | copy-start | bytes 3538948
  164.4 3.6 copy-start.7
  174.4 7.2 %copy-start.18 = (bf16[12,64,197]{2,1,0:T(8,128)(2,1)S(1)}, bf16[12,64,197]{2,1,0:T(8,128)(2,1)}, u32[]{:S(2)}) copy-start(bf16[12,64,197]{2,1,0:T(8,128)(2,1)} %copy-done.17) | copy-start | bytes 907780
  179.2 48.5 %copy-start.48 = (f32[197]{0:T(256)S(1)}, f32[197]{0:T(256)}, u32[]{:S(2)}) copy-start(f32[197]{0:T(256)} %copy-done.47) | copy-start | bytes 2368
  233.2 142.3 %all-gather.25.cloned.1.call-start = ((), (), s32[]{:S(2)}) async-start(), calls=%async_computation.14 | async-start | bytes 1622016 | tf_op jit(solution)/shard_map/all_gather | solution.py:311
  234.4 14.0 %copy-start.31 = (bf16[1,768,1536]{2,1,0:T(8,128)(2,1)S(1)}, bf16[1,768,1536]{2,1,0:T(8,128)(2,1)}, u32[]{:S(2)}) copy-start(bf16[1,768,1536]{2,1,0:T(8,128)(2,1)} %param.29) | copy-start | bytes 7077892
  234.4 14.0 %copy-start.33 = (bf16[800,768]{1,0:T(8,128)(2,1)S(1)}, bf16[800,768]{1,0:T(8,128)(2,1)}, u32[]{:S(2)}) copy-start(bf16[800,768]{1,0:T(8,128)(2,1)} %all-gather.19.cloned.1.call-done) | copy-start | bytes 3686404
  248.4 4.2 copy-start.12
  252.6 8.4 %copy-start.10 = (bf16[800,1536]{1,0:T(8,128)(2,1)}, bf16[800,1536]{1,0:T(8,128)(2,1)S(1)}, u32[]{:S(2)}) copy-start(bf16[800,1536]{1,0:T(8,128)(2,1)S(1)} %fusion.9) | copy-start | bytes 7372804
  252.6 8.4 %copy-start.8 = (bf16[1,197,3,12,64]{1,4,3,2,0:T(8,128)(2,1)S(1)}, bf16[1,197,3,12,64]{1,4,3,2,0:T(8,128)(2,1)}, u32[]{:S(2)}) copy-start(bf16[1,197,3,12,64]{1,4,3,2,0:T(8,128)(2,1)} %pad_maximum_fusion.2) | copy-start | bytes 2723332
  252.6 8.4 %copy-start.64 = (bf16[768,2304]{1,0:T(8,128)(2,1)S(1)}, bf16[768,2304]{1,0:T(8,128)(2,1)}, u32[]{:S(2)}) copy-start(bf16[768,2304]{1,0:T(8,128)(2,1)} %all-gather.11.cloned.1.call-done) | copy-start | bytes 10616836
  316.9 99.6 %all-reduce.3.cloned.1.call-start = ((), (), s32[]{:S(2)}) async-start(), calls=%async_computation.11 | async-start | bytes 1179648 | tf_op jit(solution)/shard_map/psum | solution.py:310
  322.3 9.9 %copy-start.11 = (bf16[800,1536]{1,0:T(8,128)(2,1)S(1)}, bf16[800,1536]{1,0:T(8,128)(2,1)}, u32[]{:S(2)}) copy-start(bf16[800,1536]{1,0:T(8,128)(2,1)} %copy-done.10) | copy-start | bytes 7372804
  322.3 18.4 %collective-permute-start.1 = (bf16[192,1536]{1,0:T(8,128)(2,1)}, bf16[192,1536]{1,0:T(8,128)(2,1)S(1)}, u32[]{:S(2)}, u32[]{:S(2)}) collective-permute-start(bf16[192,1536]{1,0:T(8,128)(2,1)} %get-tuple-element.64), channel_id=1, source_target_pairs={{0,8},{8,24},{16,0},{24,16},{1,9},{9,25},{17,1},{25,17},{2,10},{10... | collective-permute-start | bytes 1769480 | tf_op jit(solution)/shard_map/ppermute | solution.py:351
  323.5 17.2 %collective-permute-start = (bf16[192,1536]{1,0:T(8,128)(2,1)}, bf16[192,1536]{1,0:T(8,128)(2,1)}, u32[]{:S(2)}, u32[]{:S(2)}) collective-permute-start(bf16[192,1536]{1,0:T(8,128)(2,1)} %get-tuple-element.65), channel_id=1, source_target_pairs={{0,0},{8,16},{16,8},{24,24},{1,1},{9,17},{17,9},{25,25},{2,2},{10,... | collective-permute-start | bytes 1769480 | tf_op jit(solution)/shard_map/ppermute | solution.py:346
  332.3 3.6 copy-start.3
  338.1 104.5 %all-gather.23.cloned.1.call-start = ((), (), s32[]{:S(2)}) async-start(), calls=%async_computation.13 | async-start | bytes 1327104 | tf_op jit(solution)/shard_map/all_gather | solution.py:322
  339.2 77.3 %copy-start.28 = (f32[96,768]{1,0:T(8,128)S(1)}, f32[96,768]{1,0:T(8,128)}, u32[]{:S(2)}) copy-start(f32[96,768]{1,0:T(8,128)} %param.33) | copy-start | bytes 884740
  344.0 74.9 %copy-start.40 = (f32[768,8]{0,1:T(8,128)S(1)}, f32[768,8]{0,1:T(8,128)}, u32[]{:S(2)}) copy-start(f32[768,8]{0,1:T(8,128)} %param.31) | copy-start | bytes 73732
  344.0 77.7 %copy-start.25 = (f32[96,2304]{1,0:T(8,128)S(1)}, f32[96,2304]{1,0:T(8,128)}, u32[]{:S(2)}) copy-start(f32[96,2304]{1,0:T(8,128)} %param.32) | copy-start | bytes 2654212
  416.5 5.2 copy-start.13
  418.5 60.3 %all-gather.21.cloned.1.call-start = ((), (), s32[]{:S(2)}) async-start(), calls=%async_computation.12 | async-start | bytes 3981312 | tf_op jit(solution)/shard_map/all_gather | solution.py:321
  420.1 3.6 copy-start.34
  421.7 3.5 copy-start.37
  421.7 3.5 copy-start.39
  445.8 3.9 copy-start.22
  543.4 6.1 %copy-start.16 = (bf16[96,2304]{1,0:T(8,128)(2,1)S(1)}, bf16[96,2304]{1,0:T(8,128)(2,1)}, u32[]{:S(2)}) copy-start(bf16[96,2304]{1,0:T(8,128)(2,1)} %param.25) | copy-start | bytes 1327108
  (17 other events, 30.4 us)
Sparse Core Ops, SparseCore 0:
  9.9 36.5 all-gather.10
  48.4 23.9 all-gather.12
  74.5 89.3 all-gather.14
  165.9 29.5 all-gather.16
  197.4 30.2 all-gather.18
  233.3 52.9 reduce-scatter.1
  317.0 58.4 all-gather.24
  377.9 38.6 all-reduce.2
  419.0 23.5 all-gather.22
  444.9 33.8 all-gather.20
